TPU v7x, 512 devices: a whole 4x4x16 slice. The times are simulated.
512 devices in a mesh: seq: 32 (over z, x_hi), head: 16 (over x_lo, y, core).
Axes of the slice: x: 4 (x_hi: 2, x_lo: 2; x = x_hi * 2 + x_lo), y: 4, z: 16, core: 2. Of those that a mesh axis runs over, the one named last changes fastest.
Arguments:
- queries: bfloat16 [32768, 4096], P('seq', 'head'), may hold values from -6 to 6
- keys: bfloat16 [32768, 2048], P('seq', 'head'), may hold values from -6 to 6
- values: bfloat16 [32768, 2048], P('seq', 'head'), may hold values from -6 to 6
- grad_out: bfloat16 [32768, 4096], P('seq', 'head'), may hold values from -6 to 6
- starts: int32 [256], P('seq'), may hold values 0 or 1
Outputs:
- grad_queries: bfloat16 [32768, 4096], P('seq', 'head')
- grad_keys: bfloat16 [32768, 2048], P('seq', 'head')
- grad_values: bfloat16 [32768, 2048], P('seq', 'head')
Inputs may be any that keep to these rules, and one draw needn't show every extreme that they name: `starts`: blocks of 128 tokens, in storage order.
All inputs are finite; a program needn't handle non-finite values.
Results may differ from a plain program's by a relative error of at most 0.0087.
Values may be sent and summed in bfloat16 or wider, within the bound.
A program may use at most 64 MiB of HBM per device.

v0:
```python
import jax
import jax.numpy as jnp
from jax import lax
from jax.sharding import PartitionSpec as P

HEAD_SIZE = 128
WINDOW = 1024
QUERY_PER_KEY = 2
BLOCK = 128


query_scaling = 168.0 ** (-0.5)


def padded_2(shard, sides, width):
    for axis, dim in sides:
        count, length = (lax.axis_size(axis), shard.shape[dim])
        up = [(i, (i + 1) % count) for i in range(count - 1)]
        down = [(j, i) for i, j in up]
        last = lax.slice_in_dim(shard, length - width, length, axis=dim)
        first = lax.slice_in_dim(shard, 0, width, axis=dim)
        before = lax.ppermute(last, axis, up)
        after = lax.ppermute(first, axis, down)
        shard = jnp.concatenate([before, shard, after], axis=dim)
    return shard


def pack_piece(key_rows, value_rows, block_starts):
    joined = jnp.concatenate([key_rows, value_rows], axis=1)
    filler = jnp.zeros((joined.shape[1] - block_starts.shape[0],), jnp.bfloat16)
    marker = jnp.concatenate([block_starts.astype(jnp.bfloat16), filler])
    return jnp.concatenate([joined, marker[None, :]], axis=0)


def preceding_pieces(front_half, back_half, at_fold):
    stacked = jnp.stack([back_half, front_half])
    padded = padded_2(stacked, (("seq", 0),), 1)
    from_left = padded[0]
    from_right = padded[3]
    before_back = jnp.where(at_fold, front_half, from_right)
    return (from_left, before_back)


def return_grads(grad_front, grad_back, at_fold):
    fold_part = jnp.where(at_fold, grad_back, 0.0)
    sent_back = jnp.where(at_fold, 0.0, grad_back)
    stacked = jnp.stack([grad_front, sent_back])
    padded = padded_2(stacked, (("seq", 0),), 1)
    to_front = padded[3] + fold_part
    to_back = padded[0]
    return (to_front, to_back)


def piece_mask(piece_id, block_starts, length):
    counts = jnp.cumsum(block_starts)
    key_doc = jnp.repeat(counts, BLOCK)
    query_doc = key_doc[2 * length :]
    key_pos = (piece_id - 2) * length + jnp.arange(3 * length, dtype=jnp.int32)
    query_pos = piece_id * length + jnp.arange(length, dtype=jnp.int32)
    offset = query_pos[:, None] - key_pos[None, :]
    return (
        (offset >= 0)
        & (offset < WINDOW)
        & (key_pos[None, :] >= 0)
        & (query_doc[:, None] == key_doc[None, :])
    )


def half_grads(
    piece_id, query_rows_local, gradient_rows, older_piece, nearer_piece, own_piece, width
):
    length = query_rows_local.shape[0]
    blocks = length // BLOCK
    pieces = [older_piece, nearer_piece, own_piece]
    key_all = jnp.concatenate([p[:length, :width] for p in pieces])
    val_all = jnp.concatenate([p[:length, width:] for p in pieces])
    block_starts = jnp.concatenate([p[length, :blocks].astype(jnp.int32) for p in pieces])
    allowed = piece_mask(piece_id, block_starts, length)
    dq_parts = []
    dk_sum = jnp.zeros(key_all.shape, jnp.float32)
    dv_sum = jnp.zeros(val_all.shape, jnp.float32)
    for member in range(QUERY_PER_KEY):
        query_h = query_rows_local[:, member * HEAD_SIZE : (member + 1) * HEAD_SIZE]
        gradout_h = gradient_rows[:, member * HEAD_SIZE : (member + 1) * HEAD_SIZE]
        scores = (
            jnp.einsum("qd,kd->qk", query_h, key_all, preferred_element_type=jnp.float32)
            * query_scaling
        )
        masked = jnp.where(allowed, scores, -jnp.inf)
        row_max = jnp.max(masked, axis=1, keepdims=True)
        exp_terms = jnp.where(allowed, jnp.exp(scores - row_max), 0.0)
        weights = exp_terms / jnp.sum(exp_terms, axis=1, keepdims=True)
        weights_bfloat = weights.astype(jnp.bfloat16)
        dweights = jnp.einsum("qd,kd->qk", gradout_h, val_all, preferred_element_type=jnp.float32)
        row_dot = jnp.sum(weights * dweights, axis=1, keepdims=True)
        score_gradient = (weights * (dweights - row_dot)).astype(jnp.bfloat16)
        dq_parts.append(
            (
                jnp.dot(score_gradient, key_all, preferred_element_type=jnp.float32) * query_scaling
            ).astype(jnp.bfloat16)
        )
        dk_sum = (
            dk_sum
            + jnp.einsum("qk,qd->kd", score_gradient, query_h, preferred_element_type=jnp.float32)
            * query_scaling
        )
        dv_sum = dv_sum + jnp.einsum(
            "qk,qd->kd", weights_bfloat, gradout_h, preferred_element_type=jnp.float32
        )
    dk_cols = [dk_sum]
    dv_cols = [dv_sum]
    grad_q = jnp.concatenate(dq_parts, axis=1)
    grad_all = jnp.concatenate(dk_cols + dv_cols, axis=1)
    return (grad_q, grad_all[:length], grad_all[length : 2 * length], grad_all[2 * length :])


def on_device(queries, keys, values, grad_out, starts):
    length = keys.shape[0] // 2
    blocks = starts.shape[0] // 2
    width = keys.shape[1]
    seq_index = lax.axis_index("seq")
    seq_total = lax.axis_size("seq")
    at_fold = seq_index == seq_total - 1
    front_half = pack_piece(keys[:length], values[:length], starts[:blocks])
    back_half = pack_piece(keys[length:], values[length:], starts[blocks:])
    near_front, near_back = preceding_pieces(front_half, back_half, at_fold)
    far_front, far_back = preceding_pieces(near_front, near_back, at_fold)
    front_dq, front_far, front_near, front_own = half_grads(
        seq_index, queries[:length], grad_out[:length], far_front, near_front, front_half, width
    )
    back_dq, back_far, back_near, back_own = half_grads(
        2 * seq_total - 1 - seq_index,
        queries[length:],
        grad_out[length:],
        far_back,
        near_back,
        back_half,
        width,
    )
    grad_q = jnp.concatenate([front_dq, back_dq])
    up_front, up_back = return_grads(front_far, back_far, at_fold)
    to_front, to_back = return_grads(front_near + up_front, back_near + up_back, at_fold)
    total_front = front_own + to_front
    total_back = back_own + to_back
    key_gradient = jnp.concatenate([total_front[:, :width], total_back[:, :width]]).astype(
        jnp.bfloat16
    )
    value_gradient = jnp.concatenate([total_front[:, width:], total_back[:, width:]]).astype(
        jnp.bfloat16
    )
    return (grad_q, key_gradient, value_gradient)


def solution(mesh):
    in_specs = (P("seq", "head"), P("seq", "head"), P("seq", "head"), P("seq", "head"), P("seq"))
    out_specs = (P("seq", "head"), P("seq", "head"), P("seq", "head"))
    return jax.shard_map(
        on_device, mesh=mesh, in_specs=in_specs, out_specs=out_specs, check_vma=False
    )
```

profile of v0, /device:TPU:254, one launch (start us, length us, event | category | flops | bytes accessed | tf_op | source)
XLA Modules:
  0.0 160.4 jit_solution(11971516381381851053)
XLA Ops:
  0.6 0.7 convert.30
  1.4 1.1 fusion.81
  2.5 0.6 copy-done.16
  3.2 3.3 %collective-permute-start.2 = (bf16[1,513,256]{2,1,0:T(8,128)(2,1)S(1)}, bf16[1,513,256]{2,1,0:T(8,128)(2,1)S(1)}, u32[]{:S(2)}, u32[]{:S(2)}) collective-permute-start(bf16[1,513,256]{2,1,0:T(8,128)(2,1)S(1)} %maximum_bitcast_fusion), channel_id=1, source_target_pairs={{16,0},{32,16},{48,32},{64,48},{80,64},{96,80},{112,96},{128,112},... | collective-permute-start | bytes 787976 | tf_op jit(solution)/shard_map/ppermute | solution.py:23
  6.5 0.6 broadcast_compare_fusion.1
  7.1 0.6 broadcast_compare_fusion
  7.7 0.6 iota_add_fusion.3
  8.3 0.6 iota_add_fusion.2
  8.9 0.5 slice_bitcast_fusion.3
  9.5 7.4 %collective-permute-done.2 = bf16[1,513,256]{2,1,0:T(8,128)(2,1)S(1)} collective-permute-done((bf16[1,513,256]{2,1,0:T(8,128)(2,1)S(1)}, bf16[1,513,256]{2,1,0:T(8,128)(2,1)S(1)}, u32[]{:S(2)}, u32[]{:S(2)}) %collective-permute-start.2) | collective-permute-done | bytes 262688 | tf_op jit(solution)/shard_map/ppermute | solution.py:23
  16.9 3.8 %collective-permute-start = (bf16[1,513,256]{2,1,0:T(8,128)(2,1)S(1)}, bf16[1,513,256]{2,1,0:T(8,128)(2,1)S(1)}, u32[]{:S(2)}, u32[]{:S(2)}) collective-permute-start(bf16[1,513,256]{2,1,0:T(8,128)(2,1)S(1)} %get-tuple-element.22), channel_id=1, source_target_pairs={{0,16},{16,32},{32,48},{48,64},{64,80},{80,96},{96,112},{112,128},... | collective-permute-start | bytes 787976 | tf_op jit(solution)/shard_map/ppermute | solution.py:22
  20.8 3.6 %collective-permute-start.3 = (bf16[1,513,256]{2,1,0:T(8,128)(2,1)S(1)}, bf16[1,513,256]{2,1,0:T(8,128)(2,1)S(1)}, u32[]{:S(2)}, u32[]{:S(2)}) collective-permute-start(bf16[1,513,256]{2,1,0:T(8,128)(2,1)S(1)} %maximum_select_fusion), channel_id=1, source_target_pairs={{16,0},{32,16},{48,32},{64,48},{80,64},{96,80},{112,96},{128,112},... | collective-permute-start | bytes 787976 | tf_op jit(solution)/shard_map/ppermute | solution.py:23
  24.4 0.7 fusion.78
  25.1 2.5 %collective-permute-done = bf16[1,513,256]{2,1,0:T(8,128)(2,1)S(1)} collective-permute-done((bf16[1,513,256]{2,1,0:T(8,128)(2,1)S(1)}, bf16[1,513,256]{2,1,0:T(8,128)(2,1)S(1)}, u32[]{:S(2)}, u32[]{:S(2)}) %collective-permute-start) | collective-permute-done | bytes 262688 | tf_op jit(solution)/shard_map/ppermute | solution.py:22
  27.6 0.6 slice_bitcast_fusion.4
  28.2 0.7 fusion.76
  28.9 4.4 %collective-permute-done.3 = bf16[1,513,256]{2,1,0:T(8,128)(2,1)S(1)} collective-permute-done((bf16[1,513,256]{2,1,0:T(8,128)(2,1)S(1)}, bf16[1,513,256]{2,1,0:T(8,128)(2,1)S(1)}, u32[]{:S(2)}, u32[]{:S(2)}) %collective-permute-start.3) | collective-permute-done | bytes 262688 | tf_op jit(solution)/shard_map/ppermute | solution.py:23
  33.3 0.7 fusion.77
  34.2 0.2 reduce-window.13
  34.6 1.6 fusion.3
  36.2 2.4 %select_reduce_fusion.1 = (f32[512]{0:T(512)S(1)}, f32[512,1536]{0,1:T(8,128)S(1)}) fusion(s32[1536]{0:T(1024)S(1)} %broadcast_bitcast_fusion, s32[512]{0:T(512)S(1)} %broadcast_bitcast_fusion.2, pred[1536]{0:T(1024)(128)(4,1)} %broadcast_compare_fusion, s32[1536]{0:T(1024)S(1)} %iota_add_fusion, s32[512]{0:T(512)} %iota_add_fusion.2, ...), kind=kOutput, calls=%fused_computation.23 | convolution fusion | flops 210370048 | bytes 3690496 | tf_op jit(solution)/shard_map/qd,kd->qk/dot_general | solution.py:86
  38.7 2.0 %fusion.17 = f32[512]{0:T(512)S(1)} fusion(f32[512,1536]{0,1:T(8,128)S(1)} %get-tuple-element.39, f32[512]{0:T(512)S(1)} %get-tuple-element.38, s32[1536]{0:T(1024)S(1)} %broadcast_bitcast_fusion, s32[512]{0:T(512)S(1)} %broadcast_bitcast_fusion.2, pred[1536]{0:T(1024)(128)(4,1)S(1)} %copy-done.25, s32[1536]{0:T(1024)S(1)} %iota_add_fusion, s32[512]{0:T(512)S(1)} %copy-done.28), kind=kLoop, calls=%fused_computation.49 | loop fusion | flops 7863808 | bytes 3167744 | tf_op jit(solution)/shard_map/reduce_sum | solution.py:92
  40.7 3.4 %fusion.21 = f32[1536,128]{0,1:T(8,128)} fusion(bf16[1024,256]{1,0:T(8,128)(2,1)S(1)} %copy-done.39, f32[512,1536]{0,1:T(8,128)S(1)} %get-tuple-element.39, f32[512]{0:T(512)S(1)} %fusion.17, f32[512]{0:T(512)S(1)} %get-tuple-element.38, s32[512]{0:T(512)S(1)} %broadcast_bitcast_fusion.2, s32[1536]{0:T(1024)S(1)} %iota_add_fusion, s32[512]{0:T(512)S(1)} %copy-done.28, ...), kind=kOutput, calls=%fused_computation.61 | convolution fusion | flops 209977344 | bytes 4089856 | tf_op jit(solution)/shard_map/qk,qd->kd/dot_general | solution.py:107
  44.0 2.2 %multiply_reduce_fusion.1 = (f32[512]{0:T(512)S(1)}, f32[512]{0:T(512)S(1)}, f32[512,1536]{0,1:T(8,128)S(1)}) fusion(f32[512]{0:T(512)S(1)} %fusion.17, f32[512,1536]{0,1:T(8,128)S(1)} %get-tuple-element.39, f32[512]{0:T(512)S(1)} %get-tuple-element.38, s32[1536]{0:T(1024)S(1)} %broadcast_bitcast_fusion, s32[512]{0:T(512)S(1)} %broadcast_bitcast_fusion.2, ...), kind=kOutput, calls=%fused_computation.21 | convolution fusion | flops 213515264 | bytes 9992192 | tf_op jit(solution)/shard_map/qd,kd->qk/dot_general | solution.py:94
  46.3 2.8 %multiply_convert_fusion.1 = (bf16[512,1536]{0,1:T(8,128)(2,1)S(1)}, f32[512]{0:T(512)S(1)}) fusion(f32[512,1536]{0,1:T(8,128)S(1)} %get-tuple-element.40, f32[512]{0:T(512)S(1)} %get-tuple-element.8, f32[512]{0:T(512)S(1)} %fusion.17, f32[512,1536]{0,1:T(8,128)S(1)} %get-tuple-element.39, f32[512]{0:T(512)S(1)} %get-tuple-element.38, ...), kind=kLoop, calls=%fused_computation.20 | loop fusion | flops 12582400 | bytes 11038208 | tf_op jit(solution)/shard_map/convert_element_type | solution.py:96
  49.1 1.9 %multiply_reduce_fusion = (f32[512]{0:T(512)S(1)}, f32[512,1536]{0,1:T(8,128)S(1)}) fusion(f32[512]{0:T(512)S(1)} %get-tuple-element.35, f32[512,1536]{0,1:T(8,128)S(1)} %fusion.3, f32[512]{0:T(512)S(1)} %get-tuple-element.9, s32[1536]{0:T(1024)S(1)} %broadcast_bitcast_fusion, s32[512]{0:T(512)S(1)} %broadcast_bitcast_fusion.2, ...), kind=kOutput, calls=%fused_computation.17 | convolution fusion | flops 211942912 | bytes 6844416 | tf_op jit(solution)/shard_map/qd,kd->qk/dot_general | solution.py:94
  51.0 0.7 fusion.48
  51.7 2.4 %multiply_convert_fusion = bf16[512,1536]{0,1:T(8,128)(2,1)S(1)} fusion(f32[512,1536]{0,1:T(8,128)S(1)} %get-tuple-element.42, f32[512]{0:T(512)S(1)} %get-tuple-element.41, f32[512]{0:T(512)S(1)} %get-tuple-element.35, f32[512,1536]{0,1:T(8,128)S(1)} %fusion.3, f32[512]{0:T(512)S(1)} %get-tuple-element.9, s32[1536]{0:T(1024)S(1)} %broadcast_bitcast_fusion, ...), kind=kLoop, calls=%fused_computation.16 | loop fusion | flops 10223616 | bytes 7888384 | tf_op jit(solution)/shard_map/convert_element_type | solution.py:96
  54.2 1.6 fusion.11
  55.7 6.1 %collective-permute-start.1 = (bf16[1,513,256]{2,1,0:T(8,128)(2,1)S(1)}, bf16[1,513,256]{2,1,0:T(8,128)(2,1)S(1)}, u32[]{:S(2)}, u32[]{:S(2)}) collective-permute-start(bf16[1,513,256]{2,1,0:T(8,128)(2,1)S(1)} %copy-done.9), channel_id=1, source_target_pairs={{0,16},{16,32},{32,48},{48,64},{64,80},{80,96},{96,112},{112,128},... | collective-permute-start | bytes 787976 | tf_op jit(solution)/shard_map/ppermute | solution.py:22
  61.8 1.1 fusion.28
  62.9 4.5 %collective-permute-done.1 = bf16[1,513,256]{2,1,0:T(8,128)(2,1)S(1)} collective-permute-done((bf16[1,513,256]{2,1,0:T(8,128)(2,1)S(1)}, bf16[1,513,256]{2,1,0:T(8,128)(2,1)S(1)}, u32[]{:S(2)}, u32[]{:S(2)}) %collective-permute-start.1) | collective-permute-done | bytes 262688 | tf_op jit(solution)/shard_map/ppermute | solution.py:22
  67.4 0.7 fusion.75
  68.1 0.6 fusion.62
  68.7 1.3 reduce-window.12
  70.1 0.8 slice_bitcast_fusion.7
  70.9 0.7 broadcast_bitcast_fusion.1
  71.7 1.6 fusion.1
  73.3 1.5 select_reduce_fusion.3
  74.8 2.0 %fusion.13 = f32[512]{0:T(512)S(1)} fusion(f32[512,1536]{0,1:T(8,128)S(1)} %get-tuple-element.44, f32[512]{0:T(512)S(1)} %get-tuple-element.43, s32[1536]{0:T(1024)S(1)} %broadcast_bitcast_fusion.1, s32[512]{0:T(512)S(1)} %broadcast_bitcast_fusion.3, pred[1536]{0:T(1024)(128)(4,1)S(1)} %copy-done.27, s32[1536]{0:T(1024)S(1)} %iota_add_fusion.1, ...), kind=kLoop, calls=%fused_computation.45 | loop fusion | flops 7863808 | bytes 3167744 | tf_op jit(solution)/shard_map/reduce_sum | solution.py:92
  76.8 2.0 %fusion.24 = f32[1536,128]{0,1:T(8,128)S(1)} fusion(bf16[1024,256]{1,0:T(8,128)(2,1)S(1)} %copy-done.40, f32[512,1536]{0,1:T(8,128)S(1)} %get-tuple-element.44, f32[512]{0:T(512)S(1)} %fusion.13, f32[512]{0:T(512)S(1)} %get-tuple-element.43, s32[512]{0:T(512)S(1)} %broadcast_bitcast_fusion.3, s32[1536]{0:T(1024)S(1)} %iota_add_fusion.1, ...), kind=kOutput, calls=%fused_computation.64 | convolution fusion | flops 209977344 | bytes 4089856 | tf_op jit(solution)/shard_map/qk,qd->kd/dot_general | solution.py:107
  78.9 2.2 %multiply_reduce_fusion.3 = (f32[512]{0:T(512)S(1)}, f32[512]{0:T(512)S(1)}, f32[512,1536]{0,1:T(8,128)S(1)}) fusion(f32[512]{0:T(512)S(1)} %fusion.13, f32[512,1536]{0,1:T(8,128)S(1)} %get-tuple-element.44, f32[512]{0:T(512)S(1)} %get-tuple-element.43, s32[1536]{0:T(1024)S(1)} %broadcast_bitcast_fusion.1, s32[512]{0:T(512)S(1)} %broadcast_bitcast_fusion.3, ...), kind=kOutput, calls=%fused_computation.29 | convolution fusion | flops 213515264 | bytes 9992192 | tf_op jit(solution)/shard_map/qd,kd->qk/dot_general | solution.py:94
  81.0 2.8 %multiply_convert_fusion.3 = (bf16[512,1536]{0,1:T(8,128)(2,1)S(1)}, f32[512]{0:T(512)S(1)}) fusion(f32[512,1536]{0,1:T(8,128)S(1)} %get-tuple-element.45, f32[512]{0:T(512)S(1)} %get-tuple-element.6, f32[512]{0:T(512)S(1)} %fusion.13, f32[512,1536]{0,1:T(8,128)S(1)} %get-tuple-element.44, f32[512]{0:T(512)S(1)} %get-tuple-element.43, ...), kind=kLoop, calls=%fused_computation.28 | loop fusion | flops 12582400 | bytes 11038208 | tf_op jit(solution)/shard_map/convert_element_type | solution.py:96
  83.9 1.9 %multiply_reduce_fusion.2 = (f32[512]{0:T(512)S(1)}, f32[512,1536]{0,1:T(8,128)S(1)}) fusion(f32[512]{0:T(512)S(1)} %get-tuple-element.33, f32[512,1536]{0,1:T(8,128)S(1)} %fusion.1, f32[512]{0:T(512)S(1)} %get-tuple-element.7, s32[1536]{0:T(1024)S(1)} %broadcast_bitcast_fusion.1, s32[512]{0:T(512)S(1)} %broadcast_bitcast_fusion.3, ...), kind=kOutput, calls=%fused_computation.25 | convolution fusion | flops 211942912 | bytes 6844416 | tf_op jit(solution)/shard_map/qd,kd->qk/dot_general | solution.py:94
  85.7 2.0 %convolution_add_fusion.2 = f32[1536,128]{0,1:T(8,128)S(1)} fusion(f32[1536,128]{0,1:T(8,128)S(1)} %fusion.24, bf16[1024,256]{1,0:T(8,128)(2,1)S(1)} %copy-done.40, f32[512,1536]{0,1:T(8,128)S(1)} %fusion.1, f32[512]{0:T(512)S(1)} %get-tuple-element.33, f32[512]{0:T(512)S(1)} %get-tuple-element.7, s32[512]{0:T(512)S(1)} %broadcast_bitcast_fusion.3, ...), kind=kOutput, calls=%fused_computation.40 | convolution fusion | flops 210173952 | bytes 4876288 | tf_op jit(solution)/shard_map/qk,qd->kd/dot_general | solution.py:107
  87.7 0.6 fusion.57
  88.4 2.4 %multiply_convert_fusion.2 = bf16[512,1536]{0,1:T(8,128)(2,1)S(1)} fusion(f32[512,1536]{0,1:T(8,128)S(1)} %get-tuple-element.47, f32[512]{0:T(512)S(1)} %get-tuple-element.46, f32[512]{0:T(512)S(1)} %get-tuple-element.33, f32[512,1536]{0,1:T(8,128)S(1)} %fusion.1, f32[512]{0:T(512)S(1)} %get-tuple-element.7, s32[1536]{0:T(1024)S(1)} %broadcast_bitcast_fusion.1, ...), kind=kLoop, calls=%fused_computation.24 | loop fusion | flops 10223616 | bytes 7888384 | tf_op jit(solution)/shard_map/convert_element_type | solution.py:96
  90.8 0.7 fusion.10
  91.6 2.3 %collective-permute-start.4 = (f32[1,512,256]{1,2,0:T(8,128)S(1)}, f32[1,512,256]{1,2,0:T(8,128)S(1)}, u32[]{:S(2)}, u32[]{:S(2)}) collective-permute-start(f32[1,512,256]{1,2,0:T(8,128)S(1)} %fusion.41), channel_id=1, source_target_pairs={{16,0},{32,16},{48,32},{64,48},{80,64},{96,80},{112,96},{128,112},... | collective-permute-start | bytes 1572872 | tf_op jit(solution)/shard_map/ppermute | solution.py:23
  93.9 2.0 %convolution_add_fusion = f32[1536,128]{0,1:T(8,128)S(1)} fusion(f32[1536,128]{0,1:T(8,128)S(1)} %copy-done.41, bf16[1024,256]{1,0:T(8,128)(2,1)S(1)} %copy-done.40, f32[512,1536]{0,1:T(8,128)S(1)} %fusion.3, f32[512]{0:T(512)S(1)} %copy-done.36, f32[512]{0:T(512)S(1)} %copy-done.34, s32[512]{0:T(512)S(1)} %copy-done.32, s32[1536]{0:T(1024)S(1)} %iota_add_fusion, ...), kind=kOutput, calls=%fused_computation.38 | convolution fusion | flops 210173952 | bytes 4876288 | tf_op jit(solution)/shard_map/qk,qd->kd/dot_general | solution.py:107
  95.9 15.0 %collective-permute-done.4 = f32[1,512,256]{1,2,0:T(8,128)S(1)} collective-permute-done((f32[1,512,256]{1,2,0:T(8,128)S(1)}, f32[1,512,256]{1,2,0:T(8,128)S(1)}, u32[]{:S(2)}, u32[]{:S(2)}) %collective-permute-start.4) | collective-permute-done | bytes 524320 | tf_op jit(solution)/shard_map/ppermute | solution.py:23
  111.1 1.9 %collective-permute-start.5 = (f32[1,512,256]{1,2,0:T(8,128)S(1)}, f32[1,512,256]{1,2,0:T(8,128)S(1)}, u32[]{:S(2)}, u32[]{:S(2)}) collective-permute-start(f32[1,512,256]{1,2,0:T(8,128)S(1)} %get-tuple-element.12), channel_id=1, source_target_pairs={{16,0},{32,16},{48,32},{64,48},{80,64},{96,80},{112,96},{128,112},... | collective-permute-start | bytes 1572872 | tf_op jit(solution)/shard_map/ppermute | solution.py:23
  113.0 7.5 %collective-permute-start.6 = (f32[1,512,256]{1,2,0:T(8,128)S(1)}, f32[1,512,256]{1,2,0:T(8,128)S(1)}, u32[]{:S(2)}, u32[]{:S(2)}) collective-permute-start(f32[1,512,256]{1,2,0:T(8,128)S(1)} %get-tuple-element.13), channel_id=1, source_target_pairs={{0,16},{16,32},{32,48},{48,64},{64,80},{80,96},{96,112},{112,128},... | collective-permute-start | bytes 1572872 | tf_op jit(solution)/shard_map/ppermute | solution.py:22
  120.6 0.4 fusion.29
  121.0 0.4 fusion.26
  121.5 12.9 %collective-permute-done.5 = f32[1,512,256]{1,2,0:T(8,128)S(1)} collective-permute-done((f32[1,512,256]{1,2,0:T(8,128)S(1)}, f32[1,512,256]{1,2,0:T(8,128)S(1)}, u32[]{:S(2)}, u32[]{:S(2)}) %collective-permute-start.5) | collective-permute-done | bytes 524320 | tf_op jit(solution)/shard_map/ppermute | solution.py:23
  134.4 5.7 %collective-permute-done.6 = f32[1,512,256]{1,2,0:T(8,128)S(1)} collective-permute-done((f32[1,512,256]{1,2,0:T(8,128)S(1)}, f32[1,512,256]{1,2,0:T(8,128)S(1)}, u32[]{:S(2)}, u32[]{:S(2)}) %collective-permute-start.6) | collective-permute-done | bytes 524320 | tf_op jit(solution)/shard_map/ppermute | solution.py:22
  140.0 1.1 fusion.38
  141.1 3.1 %collective-permute-start.7 = (f32[1,512,256]{1,2,0:T(8,128)}, f32[1,512,256]{1,2,0:T(8,128)S(1)}, u32[]{:S(2)}, u32[]{:S(2)}) collective-permute-start(f32[1,512,256]{1,2,0:T(8,128)} %get-tuple-element.11), channel_id=1, source_target_pairs={{0,16},{16,32},{32,48},{48,64},{64,80},{80,96},{96,112},{112,128},... | collective-permute-start | bytes 1572872 | tf_op jit(solution)/shard_map/ppermute | solution.py:22
  144.2 0.4 fusion.27
  144.7 1.0 copy.8
  145.7 12.8 %collective-permute-done.7 = f32[1,512,256]{1,2,0:T(8,128)S(1)} collective-permute-done((f32[1,512,256]{1,2,0:T(8,128)}, f32[1,512,256]{1,2,0:T(8,128)S(1)}, u32[]{:S(2)}, u32[]{:S(2)}) %collective-permute-start.7) | collective-permute-done | bytes 524320 | tf_op jit(solution)/shard_map/ppermute | solution.py:22
  158.6 0.8 copy.10
  159.5 0.8 copy.9
  (113 shorter events, 1.3 us)
Async XLA Ops:
  2.5 0.7 copy-start.16
  3.2 13.6 %collective-permute-start.2 = (bf16[1,513,256]{2,1,0:T(8,128)(2,1)S(1)}, bf16[1,513,256]{2,1,0:T(8,128)(2,1)S(1)}, u32[]{:S(2)}, u32[]{:S(2)}) collective-permute-start(bf16[1,513,256]{2,1,0:T(8,128)(2,1)S(1)} %maximum_bitcast_fusion), channel_id=1, source_target_pairs={{16,0},{32,16},{48,32},{64,48},{80,64},{96,80},{112,96},{128,112},... | collective-permute-start | bytes 787976 | tf_op jit(solution)/shard_map/ppermute | solution.py:23
  16.9 10.7 %collective-permute-start = (bf16[1,513,256]{2,1,0:T(8,128)(2,1)S(1)}, bf16[1,513,256]{2,1,0:T(8,128)(2,1)S(1)}, u32[]{:S(2)}, u32[]{:S(2)}) collective-permute-start(bf16[1,513,256]{2,1,0:T(8,128)(2,1)S(1)} %get-tuple-element.22), channel_id=1, source_target_pairs={{0,16},{16,32},{32,48},{48,64},{64,80},{80,96},{96,112},{112,128},... | collective-permute-start | bytes 787976 | tf_op jit(solution)/shard_map/ppermute | solution.py:22
  20.8 12.5 %collective-permute-start.3 = (bf16[1,513,256]{2,1,0:T(8,128)(2,1)S(1)}, bf16[1,513,256]{2,1,0:T(8,128)(2,1)S(1)}, u32[]{:S(2)}, u32[]{:S(2)}) collective-permute-start(bf16[1,513,256]{2,1,0:T(8,128)(2,1)S(1)} %maximum_select_fusion), channel_id=1, source_target_pairs={{16,0},{32,16},{48,32},{64,48},{80,64},{96,80},{112,96},{128,112},... | collective-permute-start | bytes 787976 | tf_op jit(solution)/shard_map/ppermute | solution.py:23
  27.6 7.0 %copy-start.8 = (bf16[1,513,256]{2,1,0:T(8,128)(2,1)}, bf16[1,513,256]{2,1,0:T(8,128)(2,1)S(1)}, u32[]{:S(2)}) copy-start(bf16[1,513,256]{2,1,0:T(8,128)(2,1)S(1)} %collective-permute-done) | copy-start | bytes 787972
  34.3 1.8 %copy-start.11 = (bf16[512,128]{1,0:T(8,128)(2,1)S(1)}, bf16[512,128]{1,0:T(8,128)(2,1)}, u32[]{:S(2)}) copy-start(bf16[512,128]{1,0:T(8,128)(2,1)} %get-tuple-element.20) | copy-start | bytes 393220
  34.3 1.8 %copy-start.13 = (bf16[512,128]{1,0:T(8,128)(2,1)S(1)}, bf16[512,128]{1,0:T(8,128)(2,1)}, u32[]{:S(2)}) copy-start(bf16[512,128]{1,0:T(8,128)(2,1)} %get-tuple-element.18) | copy-start | bytes 393220
  34.5 17.2 %copy-start.23 = (s32[1536]{0:T(1024)}, s32[1536]{0:T(1024)S(1)}, u32[]{:S(2)}) copy-start(s32[1536]{0:T(1024)S(1)} %broadcast_bitcast_fusion) | copy-start | bytes 18436
  34.6 17.1 %copy-start.31 = (s32[512]{0:T(512)}, s32[512]{0:T(512)S(1)}, u32[]{:S(2)}) copy-start(s32[512]{0:T(512)S(1)} %broadcast_bitcast_fusion.2) | copy-start | bytes 6148
  36.2 2.4 %copy-start.25 = (pred[1536]{0:T(1024)(128)(4,1)S(1)}, pred[1536]{0:T(1024)(128)(4,1)}, u32[]{:S(2)}) copy-start(pred[1536]{0:T(1024)(128)(4,1)} %broadcast_compare_fusion) | copy-start | bytes 4612
  36.2 2.4 %copy-start.28 = (s32[512]{0:T(512)S(1)}, s32[512]{0:T(512)}, u32[]{:S(2)}) copy-start(s32[512]{0:T(512)} %iota_add_fusion.2) | copy-start | bytes 6148
  38.6 2.0 %copy-start.39 = (bf16[1024,256]{1,0:T(8,128)(2,1)S(1)}, bf16[1024,256]{1,0:T(8,128)(2,1)}, u32[]{:S(2)}) copy-start(bf16[1024,256]{1,0:T(8,128)(2,1)} %param.8) | copy-start | bytes 1572868
  40.6 3.4 %copy-start.17 = (bf16[512,128]{1,0:T(8,128)(2,1)S(1)}, bf16[512,128]{1,0:T(8,128)(2,1)}, u32[]{:S(2)}) copy-start(bf16[512,128]{1,0:T(8,128)(2,1)} %copy-done.16) | copy-start | bytes 393220
  40.6 3.4 %copy-start.19 = (bf16[512,128]{1,0:T(8,128)(2,1)S(1)}, bf16[512,128]{1,0:T(8,128)(2,1)}, u32[]{:S(2)}) copy-start(bf16[512,128]{1,0:T(8,128)(2,1)} %get-tuple-element.21) | copy-start | bytes 393220
  40.7 3.4 %copy-start.21 = (bf16[512,128]{1,0:T(8,128)(2,1)S(1)}, bf16[512,128]{1,0:T(8,128)(2,1)}, u32[]{:S(2)}) copy-start(bf16[512,128]{1,0:T(8,128)(2,1)} %get-tuple-element.19) | copy-start | bytes 393220
  46.2 5.5 %copy-start.33 = (f32[512]{0:T(512)}, f32[512]{0:T(512)S(1)}, u32[]{:S(2)}) copy-start(f32[512]{0:T(512)S(1)} %get-tuple-element.9) | copy-start | bytes 6148
  49.1 2.6 %copy-start.35 = (f32[512]{0:T(512)}, f32[512]{0:T(512)S(1)}, u32[]{:S(2)}) copy-start(f32[512]{0:T(512)S(1)} %get-tuple-element.35) | copy-start | bytes 6148
  49.1 1.9 %copy-start.6 = (bf16[1024,256]{1,0:T(8,128)(2,1)S(1)}, bf16[1024,256]{1,0:T(8,128)(2,1)}, u32[]{:S(2)}) copy-start(bf16[1024,256]{1,0:T(8,128)(2,1)} %param.5) | copy-start | bytes 1572868
  54.1 8.8 %copy-start.4 = (bf16[512,1536]{0,1:T(8,128)(2,1)}, bf16[512,1536]{0,1:T(8,128)(2,1)S(1)}, u32[]{:S(2)}) copy-start(bf16[512,1536]{0,1:T(8,128)(2,1)S(1)} %multiply_convert_fusion) | copy-start | bytes 4718596
  54.1 1.6 copy-start.9
  54.1 14.0 %copy-start.37 = (bf16[4]{0:T(256)(128)(2,1)S(1)}, bf16[4]{0:T(256)(128)(2,1)}, u32[]{:S(2)}) copy-start(bf16[4]{0:T(256)(128)(2,1)} %slice_bitcast_fusion.3) | copy-start | bytes 28
  54.2 14.0 %copy-start.38 = (bf16[4]{0:T(256)(128)(2,1)S(1)}, bf16[4]{0:T(256)(128)(2,1)}, u32[]{:S(2)}) copy-start(bf16[4]{0:T(256)(128)(2,1)} %slice_bitcast_fusion.4) | copy-start | bytes 28
  55.7 11.7 %collective-permute-start.1 = (bf16[1,513,256]{2,1,0:T(8,128)(2,1)S(1)}, bf16[1,513,256]{2,1,0:T(8,128)(2,1)S(1)}, u32[]{:S(2)}, u32[]{:S(2)}) collective-permute-start(bf16[1,513,256]{2,1,0:T(8,128)(2,1)S(1)} %copy-done.9), channel_id=1, source_target_pairs={{0,16},{16,32},{32,48},{48,64},{64,80},{80,96},{96,112},{112,128},... | collective-permute-start | bytes 787976 | tf_op jit(solution)/shard_map/ppermute | solution.py:22
  70.1 3.2 %copy-start.7 = (bf16[1024,256]{1,0:T(8,128)(2,1)S(1)}, bf16[1024,256]{1,0:T(8,128)(2,1)}, u32[]{:S(2)}) copy-start(bf16[1024,256]{1,0:T(8,128)(2,1)} %param.5) | copy-start | bytes 1572868
  70.1 3.2 %copy-start.10 = (bf16[512,128]{1,0:T(8,128)(2,1)S(1)}, bf16[512,128]{1,0:T(8,128)(2,1)}, u32[]{:S(2)}) copy-start(bf16[512,128]{1,0:T(8,128)(2,1)} %get-tuple-element.16) | copy-start | bytes 393220
  70.1 3.2 %copy-start.15 = (bf16[512,128]{1,0:T(8,128)(2,1)S(1)}, bf16[512,128]{1,0:T(8,128)(2,1)}, u32[]{:S(2)}) copy-start(bf16[512,128]{1,0:T(8,128)(2,1)} %get-tuple-element.14) | copy-start | bytes 393220
  70.1 3.3 %copy-start.27 = (pred[1536]{0:T(1024)(128)(4,1)S(1)}, pred[1536]{0:T(1024)(128)(4,1)}, u32[]{:S(2)}) copy-start(pred[1536]{0:T(1024)(128)(4,1)} %broadcast_compare_fusion.1) | copy-start | bytes 4612
  70.1 3.3 %copy-start.30 = (s32[512]{0:T(512)S(1)}, s32[512]{0:T(512)}, u32[]{:S(2)}) copy-start(s32[512]{0:T(512)} %iota_add_fusion.3) | copy-start | bytes 6148
  74.8 2.0 %copy-start.40 = (bf16[1024,256]{1,0:T(8,128)(2,1)S(1)}, bf16[1024,256]{1,0:T(8,128)(2,1)}, u32[]{:S(2)}) copy-start(bf16[1024,256]{1,0:T(8,128)(2,1)} %param.8) | copy-start | bytes 1572868
  76.8 2.0 %copy-start.18 = (bf16[512,128]{1,0:T(8,128)(2,1)S(1)}, bf16[512,128]{1,0:T(8,128)(2,1)}, u32[]{:S(2)}) copy-start(bf16[512,128]{1,0:T(8,128)(2,1)} %get-tuple-element.17) | copy-start | bytes 393220
  76.8 2.0 %copy-start.20 = (bf16[512,128]{1,0:T(8,128)(2,1)S(1)}, bf16[512,128]{1,0:T(8,128)(2,1)}, u32[]{:S(2)}) copy-start(bf16[512,128]{1,0:T(8,128)(2,1)} %get-tuple-element.15) | copy-start | bytes 393220
  90.8 3.1 %copy-start.24 = (s32[1536]{0:T(1024)S(1)}, s32[1536]{0:T(1024)}, u32[]{:S(2)}) copy-start(s32[1536]{0:T(1024)} %copy-done.23) | copy-start | bytes 18436
  90.8 3.1 %copy-start.26 = (pred[1536]{0:T(1024)(128)(4,1)S(1)}, pred[1536]{0:T(1024)(128)(4,1)}, u32[]{:S(2)}) copy-start(pred[1536]{0:T(1024)(128)(4,1)} %broadcast_compare_fusion) | copy-start | bytes 4612
  90.8 3.1 %copy-start.29 = (s32[512]{0:T(512)S(1)}, s32[512]{0:T(512)}, u32[]{:S(2)}) copy-start(s32[512]{0:T(512)} %iota_add_fusion.2) | copy-start | bytes 6148
  90.8 3.1 %copy-start.32 = (s32[512]{0:T(512)S(1)}, s32[512]{0:T(512)}, u32[]{:S(2)}) copy-start(s32[512]{0:T(512)} %copy-done.31) | copy-start | bytes 6148
  90.8 3.1 %copy-start.34 = (f32[512]{0:T(512)S(1)}, f32[512]{0:T(512)}, u32[]{:S(2)}) copy-start(f32[512]{0:T(512)} %copy-done.33) | copy-start | bytes 6148
  90.8 3.1 %copy-start.36 = (f32[512]{0:T(512)S(1)}, f32[512]{0:T(512)}, u32[]{:S(2)}) copy-start(f32[512]{0:T(512)} %copy-done.35) | copy-start | bytes 6148
  90.8 3.1 %copy-start.41 = (f32[1536,128]{0,1:T(8,128)S(1)}, f32[1536,128]{0,1:T(8,128)}, u32[]{:S(2)}) copy-start(f32[1536,128]{0,1:T(8,128)} %fusion.21) | copy-start | bytes 2359300
  91.5 19.4 %copy-start = (f32[1536,128]{0,1:T(8,128)S(1)}, f32[1536,128]{0,1:T(8,128)}, u32[]{:S(2)}) copy-start(f32[1536,128]{0,1:T(8,128)} %fusion.11) | copy-start | bytes 2359300
  91.6 19.4 %collective-permute-start.4 = (f32[1,512,256]{1,2,0:T(8,128)S(1)}, f32[1,512,256]{1,2,0:T(8,128)S(1)}, u32[]{:S(2)}, u32[]{:S(2)}) collective-permute-start(f32[1,512,256]{1,2,0:T(8,128)S(1)} %fusion.41), channel_id=1, source_target_pairs={{16,0},{32,16},{48,32},{64,48},{80,64},{96,80},{112,96},{128,112},... | collective-permute-start | bytes 1572872 | tf_op jit(solution)/shard_map/ppermute | solution.py:23
  95.9 44.1 %copy-start.2 = (f32[1536,128]{0,1:T(8,128)}, f32[1536,128]{0,1:T(8,128)S(1)}, u32[]{:S(2)}) copy-start(f32[1536,128]{0,1:T(8,128)S(1)} %convolution_add_fusion) | copy-start | bytes 2359300
  95.9 24.7 %copy-start.5 = (bf16[512,1536]{0,1:T(8,128)(2,1)S(1)}, bf16[512,1536]{0,1:T(8,128)(2,1)}, u32[]{:S(2)}) copy-start(bf16[512,1536]{0,1:T(8,128)(2,1)} %copy-done.4) | copy-start | bytes 4718596
  95.9 24.7 %copy-start.12 = (bf16[512,128]{1,0:T(8,128)(2,1)S(1)}, bf16[512,128]{1,0:T(8,128)(2,1)}, u32[]{:S(2)}) copy-start(bf16[512,128]{1,0:T(8,128)(2,1)} %get-tuple-element.20) | copy-start | bytes 393220
  95.9 24.7 %copy-start.14 = (bf16[512,128]{1,0:T(8,128)(2,1)S(1)}, bf16[512,128]{1,0:T(8,128)(2,1)}, u32[]{:S(2)}) copy-start(bf16[512,128]{1,0:T(8,128)(2,1)} %get-tuple-element.18) | copy-start | bytes 393220
  111.1 23.3 %collective-permute-start.5 = (f32[1,512,256]{1,2,0:T(8,128)S(1)}, f32[1,512,256]{1,2,0:T(8,128)S(1)}, u32[]{:S(2)}, u32[]{:S(2)}) collective-permute-start(f32[1,512,256]{1,2,0:T(8,128)S(1)} %get-tuple-element.12), channel_id=1, source_target_pairs={{16,0},{32,16},{48,32},{64,48},{80,64},{96,80},{112,96},{128,112},... | collective-permute-start | bytes 1572872 | tf_op jit(solution)/shard_map/ppermute | solution.py:23
  113.0 27.0 %collective-permute-start.6 = (f32[1,512,256]{1,2,0:T(8,128)S(1)}, f32[1,512,256]{1,2,0:T(8,128)S(1)}, u32[]{:S(2)}, u32[]{:S(2)}) collective-permute-start(f32[1,512,256]{1,2,0:T(8,128)S(1)} %get-tuple-element.13), channel_id=1, source_target_pairs={{0,16},{16,32},{32,48},{48,64},{64,80},{80,96},{96,112},{112,128},... | collective-permute-start | bytes 1572872 | tf_op jit(solution)/shard_map/ppermute | solution.py:22
  141.1 3.5 %copy-start.22 = (bf16[512,128]{0,1:T(8,128)(2,1)S(1)}, bf16[512,128]{0,1:T(8,128)(2,1)}, u32[]{:S(2)}) copy-start(bf16[512,128]{0,1:T(8,128)(2,1)} %fusion.28) | copy-start | bytes 393220
  141.1 17.4 %copy-start.1 = (f32[1536,128]{0,1:T(8,128)S(1)}, f32[1536,128]{0,1:T(8,128)}, u32[]{:S(2)}) copy-start(f32[1536,128]{0,1:T(8,128)} %fusion.11) | copy-start | bytes 2359300
  141.1 17.4 %copy-start.3 = (f32[1536,128]{0,1:T(8,128)S(1)}, f32[1536,128]{0,1:T(8,128)}, u32[]{:S(2)}) copy-start(f32[1536,128]{0,1:T(8,128)} %copy-done.2) | copy-start | bytes 2359300
  141.1 17.4 %collective-permute-start.7 = (f32[1,512,256]{1,2,0:T(8,128)}, f32[1,512,256]{1,2,0:T(8,128)S(1)}, u32[]{:S(2)}, u32[]{:S(2)}) collective-permute-start(f32[1,512,256]{1,2,0:T(8,128)} %get-tuple-element.11), channel_id=1, source_target_pairs={{0,16},{16,32},{32,48},{48,64},{64,80},{80,96},{96,112},{112,128},... | collective-permute-start | bytes 1572872 | tf_op jit(solution)/shard_map/ppermute | solution.py:22
where the time goes:
time: 161 us; the launch traced here: 160 us
  waiting for transfers between devices  65.2 us (40%)
  starting transfers between devices  31.5 us (20%)
  matrix products  30.5 us (19%)
  other arithmetic  21.2 us (13%)
  local copies, waits for them, and re-layouts  10.6 us (7%)
    ppermute x4, waiting for transfers between devices, padded_2(): after = lax.ppermute(first, axis, down)  39.7 us
    ppermute x4, waiting for transfers between devices, padded_2(): before = lax.ppermute(last, axis, up)  25.5 us
    ppermute x4, starting transfers between devices, padded_2(): before = lax.ppermute(last, axis, up)  20.4 us
    ppermute x4, starting transfers between devices, padded_2(): after = lax.ppermute(first, axis, down)  11.1 us
    convert_element_type x4, other arithmetic, half_grads(): score_gradient = (weights * (dweights - row_dot)).astype(jnp.bfloat16)  10.4 us
    dot_general x4, matrix products, half_grads(): jnp.einsum('qk,qd->kd', weights_bfloat, gradout_h, preferred_element_type...  9.34 us
    dot_general x4, matrix products, half_grads(): jnp.einsum('qd,kd->qk', gradout_h, val_all, preferred_element_type=jnp.fl...  8.13 us
    dot_general x4, matrix products, half_grads(): jnp.einsum('qd,kd->qk', query_h, key_all, preferred_element_type=jnp.floa...  7.09 us
  transfers between devices with their start and end apart: 8, of which 8 were waited for; matrix products, arithmetic and copies ran while one was open for 7% of the time, Pallas kernels for 0%

commit v1 on v0

v1 whole, which is shorter than its diff:
```python
import functools

import jax
import jax.numpy as jnp
from jax import lax
from jax.experimental import pallas as pl
from jax.experimental.pallas import tpu as pltpu
from jax.sharding import PartitionSpec as P

HEAD_SIZE = 128
BLOCK = 128
PIECE = 512
BLOCKS = PIECE // BLOCK
HEADS = 2
TILE = HEADS * BLOCK
LANES = BLOCKS * TILE
OWN, NEAR, FAR = 0, 1, 2
MASKED = -1e30
MESH = pl.DeviceIdType.MESH

query_scaling = 168.0 ** (-0.5)
exp2_scaling = query_scaling * 1.4426950408889634


def span(chunk, i):
    if chunk == OWN:
        return range(i + 1)
    if chunk == FAR:
        return range(i, BLOCKS)
    return range(BLOCKS)


def rows_of(j):
    return slice(j * BLOCK, (j + 1) * BLOCK)


def lanes_of(i):
    return slice(i * TILE, (i + 1) * TILE)


def last_dims(a, b):
    return lax.dot_general(a, b, (((1,), (1,)), ((), ())), preferred_element_type=jnp.float32)


def kernel(
    n, q_hbm, g_hbm, k_hbm, v_hbm, starts, dq_hbm, dk_hbm, dv_hbm,
    q_in, g_in, k_all, v_all, k_t, table, tables, q_cat, g_cat, terms, dweights, dscores, stats,
    grads_out, grads_in, grads_own, dq_out, dk_out, dv_out,
    load_sem, store_sem, k_send, v_send, t_send, k_recv, v_recv, t_recv, g_send, g_recv,
):
    s = lax.axis_index("seq")
    head = lax.axis_index("head")

    loads = [
        pltpu.make_async_copy(q_hbm, q_in, load_sem.at[0]),
        pltpu.make_async_copy(g_hbm, g_in, load_sem.at[1]),
    ]
    for half in range(2):
        piece = pl.ds(half * PIECE, PIECE)
        loads.append(pltpu.make_async_copy(k_hbm.at[piece], k_all.at[half, OWN], load_sem.at[2 + 2 * half]))
        loads.append(pltpu.make_async_copy(v_hbm.at[piece], v_all.at[half, OWN], load_sem.at[3 + 2 * half]))
    for copy in loads:
        copy.start()

    barrier = pltpu.get_barrier_semaphore()
    for step in (-2, -1, 1, 2):
        there = s + step

        @pl.when((there >= 0) & (there < n))
        def _():
            pl.semaphore_signal(barrier, inc=1, device_id=(there, head), device_id_type=MESH)

    for half in range(2):
        own = [starts[half * BLOCKS + j].astype(jnp.float32) for j in range(BLOCKS)]
        line = lax.broadcasted_iota(jnp.int32, (8, BLOCK), 0)
        after = jnp.zeros((8, BLOCK), jnp.float32)
        for j in range(BLOCKS):
            after = after + jnp.where((line < j) | (line == BLOCKS), own[j], 0.0)
        table[half] = after

    @pl.when(s == 0)
    def _():
        k_all[0, NEAR] = jnp.zeros((PIECE, HEAD_SIZE), jnp.bfloat16)
        v_all[0, NEAR] = jnp.zeros((PIECE, HEAD_SIZE), jnp.bfloat16)
        tables[0, NEAR] = jnp.ones((8, BLOCK), jnp.float32)
        grads_in[1, NEAR] = jnp.zeros((PIECE, 2 * HEAD_SIZE), jnp.bfloat16)

    @pl.when(s <= 1)
    def _():
        k_all[0, FAR] = jnp.zeros((PIECE, HEAD_SIZE), jnp.bfloat16)
        v_all[0, FAR] = jnp.zeros((PIECE, HEAD_SIZE), jnp.bfloat16)
        tables[0, FAR] = jnp.ones((8, BLOCK), jnp.float32)
        grads_in[1, FAR] = jnp.zeros((PIECE, 2 * HEAD_SIZE), jnp.bfloat16)

    pl.semaphore_wait(barrier, jnp.minimum(s, 2) + jnp.minimum(n - 1 - s, 2))

    folded = s > n - 3
    beyond = jnp.where(folded, 2 * n - 3 - s, s + 2)
    other_half = jnp.where(folded, 1, 0)
    same_half = jnp.where(folded, 0, 1)

    def pass_piece(half, slot, there, to_half):
        piece = pl.ds(half * PIECE, PIECE)
        target = dict(device_id=(there, head), device_id_type=MESH)
        at = (half, slot - 1)
        to = (to_half, slot - 1)
        return [
            pltpu.make_async_remote_copy(
                table.at[half], tables.at[to_half, slot], t_send.at[at], t_recv.at[to], **target),
            pltpu.make_async_remote_copy(
                k_hbm.at[piece], k_all.at[to_half, slot], k_send.at[at], k_recv.at[to], **target),
            pltpu.make_async_remote_copy(
                v_hbm.at[piece], v_all.at[to_half, slot], v_send.at[at], v_recv.at[to], **target),
        ]

    def pass_grads(half, slot, there, to_half):
        return pltpu.make_async_remote_copy(
            grads_out.at[half, slot - 1], grads_in.at[to_half, slot], g_send.at[half, slot - 1],
            g_recv.at[to_half, slot - 1], device_id=(there, head), device_id_type=MESH)

    at_fold = s == n - 1
    forward = [
        (s < n - 1, lambda: pass_piece(0, NEAR, s + 1, 0)),
        (s >= 1, lambda: pass_piece(1, NEAR, s - 1, 1)),
        (s >= 0, lambda: pass_piece(0, FAR, beyond, other_half)),
        (s >= 2, lambda: pass_piece(1, FAR, s - 2, 1)),
    ]
    across = [
        pltpu.make_async_copy(table.at[0], tables.at[1, NEAR], t_recv.at[1, 0]),
        pltpu.make_async_copy(k_hbm.at[pl.ds(0, PIECE)], k_all.at[1, NEAR], k_recv.at[1, 0]),
        pltpu.make_async_copy(v_hbm.at[pl.ds(0, PIECE)], v_all.at[1, NEAR], v_recv.at[1, 0]),
    ]
    for wanted, copies in forward:

        @pl.when(wanted)
        def _():
            for copy in copies():
                copy.start()

    @pl.when(at_fold)
    def _():
        for copy in across:
            copy.start()

    for copy in loads:
        copy.wait()

    for half in range(2):
        for i in range(BLOCKS):
            for h in range(HEADS):
                rows = slice(half * PIECE + i * BLOCK, half * PIECE + (i + 1) * BLOCK)
                to = slice(i * TILE + h * BLOCK, i * TILE + (h + 1) * BLOCK)
                cols = slice(h * HEAD_SIZE, (h + 1) * HEAD_SIZE)
                q_cat[half, to, :] = q_in[rows, cols]
                g_cat[half, to, :] = g_in[rows, cols]

    key_row = lax.broadcasted_iota(jnp.int32, (BLOCK, TILE), 0)
    query_row = lax.broadcasted_iota(jnp.int32, (BLOCK, TILE), 1) % BLOCK
    causal = key_row <= query_row

    def first_pass(half, chunk):
        k_t[half, chunk] = k_all[half, chunk].T
        for i in range(BLOCKS):
            begun = [starts[half * BLOCKS + j] for j in range(BLOCKS)]
            q_i = q_cat[half, lanes_of(i), :]
            g_i = g_cat[half, lanes_of(i), :]
            scores = []
            for j in span(chunk, i):
                x = last_dims(k_all[half, chunk, rows_of(j), :], q_i) * exp2_scaling
                if chunk == OWN:
                    count = functools.reduce(lambda a, b: a + b, begun[j + 1 : i + 1], jnp.int32(0))
                    since = jnp.full((1, BLOCK), count.astype(jnp.float32))
                else:
                    count = functools.reduce(lambda a, b: a + b, begun[: i + 1])
                    since = tables[half, chunk, j : j + 1, :] + count.astype(jnp.float32)
                    if chunk == FAR:
                        since = since + tables[half, NEAR, BLOCKS : BLOCKS + 1, :]
                if not (chunk == OWN and j == i):
                    bias = jnp.where(since > 0.5, MASKED, 0.0)
                    x = x + jnp.concatenate([bias, bias], axis=1)
                if chunk == OWN and j == i:
                    x = jnp.where(causal, x, MASKED)
                if chunk == FAR and j == i:
                    x = jnp.where(causal, MASKED, x)
                scores.append(x)
            top = functools.reduce(jnp.maximum, [jnp.max(x, axis=0, keepdims=True) for x in scores])
            total = jnp.zeros((1, TILE), jnp.float32)
            dotted = jnp.zeros((1, TILE), jnp.float32)
            for j, x in zip(span(chunk, i), scores):
                e = jnp.exp2(x - top)
                w = last_dims(v_all[half, chunk, rows_of(j), :], g_i)
                total = total + jnp.sum(e, axis=0, keepdims=True)
                dotted = dotted + jnp.sum(e * w, axis=0, keepdims=True)
                terms[half, chunk, rows_of(j), lanes_of(i)] = e
                dweights[half, chunk, rows_of(j), lanes_of(i)] = w
            stats[half, chunk, 0:1, lanes_of(i)] = top
            stats[half, chunk, 1:2, lanes_of(i)] = total
            stats[half, chunk, 2:3, lanes_of(i)] = dotted

    def merge(half):
        tops = [stats[half, c, 0:1, :] for c in range(3)]
        top = functools.reduce(jnp.maximum, tops)
        ratios = [jnp.exp2(t - top) for t in tops]
        total = sum(stats[half, c, 1:2, :] * ratios[c] for c in range(3))
        dotted = sum(stats[half, c, 2:3, :] * ratios[c] for c in range(3))
        inverse = 1.0 / total
        for c in range(3):
            stats[half, c, 3:4, :] = ratios[c] * inverse
        stats[half, OWN, 4:5, :] = dotted * inverse

    def second_pass(half, chunk):
        for j in range(BLOCKS):
            dk = jnp.zeros((BLOCK, HEAD_SIZE), jnp.float32)
            dv = jnp.zeros((BLOCK, HEAD_SIZE), jnp.float32)
            for i in range(BLOCKS):
                if j not in span(chunk, i):
                    continue
                p = terms[half, chunk, rows_of(j), lanes_of(i)] * stats[half, chunk, 3:4, lanes_of(i)]
                d = p * (dweights[half, chunk, rows_of(j), lanes_of(i)] - stats[half, OWN, 4:5, lanes_of(i)])
                d = d.astype(jnp.bfloat16)
                dscores[half, chunk, rows_of(j), lanes_of(i)] = d
                dk = dk + jnp.dot(d, q_cat[half, lanes_of(i), :], preferred_element_type=jnp.float32)
                dv = dv + jnp.dot(
                    p.astype(jnp.bfloat16), g_cat[half, lanes_of(i), :], preferred_element_type=jnp.float32)
            both = jnp.concatenate([dk * query_scaling, dv], axis=1)
            if chunk == OWN:
                grads_own[half, rows_of(j), :] = both
            else:
                grads_out[half, chunk - 1, rows_of(j), :] = both.astype(jnp.bfloat16)

    def query_pass(half):
        for i in range(BLOCKS):
            total = jnp.zeros((HEAD_SIZE, TILE), jnp.float32)
            for c in range(3):
                js = span(c, i)
                keys = slice(js[0] * BLOCK, (js[-1] + 1) * BLOCK)
                total = total + jnp.dot(
                    k_t[half, c, :, keys], dscores[half, c, keys, lanes_of(i)], preferred_element_type=jnp.float32)
            turned = (total * query_scaling).T.astype(jnp.bfloat16)
            rows = pl.ds(half * PIECE + i * BLOCK, BLOCK)
            for h in range(HEADS):
                dq_out[rows, h * HEAD_SIZE : (h + 1) * HEAD_SIZE] = turned[h * BLOCK : (h + 1) * BLOCK, :]

    def await_piece(half, slot):
        pltpu.make_async_copy(table.at[0], tables.at[half, slot], t_recv.at[half, slot - 1]).wait()
        pltpu.make_async_copy(k_hbm.at[pl.ds(0, PIECE)], k_all.at[half, slot], k_recv.at[half, slot - 1]).wait()
        pltpu.make_async_copy(v_hbm.at[pl.ds(0, PIECE)], v_all.at[half, slot], v_recv.at[half, slot - 1]).wait()

    def await_grads(half, slot):
        pltpu.make_async_copy(grads_out.at[0, 0], grads_in.at[half, slot], g_recv.at[half, slot - 1]).wait()

    for half in range(2):
        first_pass(half, OWN)

    backward = [
        [(s >= 1, lambda: pass_grads(0, NEAR, s - 1, 0)), (s >= 2, lambda: pass_grads(0, FAR, s - 2, 0))],
        [(s < n - 1, lambda: pass_grads(1, NEAR, s + 1, 1)), (s >= 0, lambda: pass_grads(1, FAR, beyond, same_half))],
    ]
    home = pltpu.make_async_copy(grads_out.at[1, 0], grads_in.at[0, NEAR], g_recv.at[0, 0])

    for half in range(2):
        for slot in (NEAR, FAR):
            if half == 1:
                await_piece(half, slot)
            else:

                @pl.when(s >= slot)
                def _():
                    await_piece(half, slot)

            first_pass(half, slot)
        merge(half)
        for slot in (NEAR, FAR):
            second_pass(half, slot)
            wanted, copy = backward[half][slot - 1]

            @pl.when(wanted)
            def _():
                copy().start()

            if half == 1 and slot == NEAR:

                @pl.when(at_fold)
                def _():
                    home.start()

    stores = []
    for half in range(2):
        second_pass(half, OWN)
        query_pass(half)
    stores.append(pltpu.make_async_copy(dq_out, dq_hbm, store_sem.at[0]))
    stores[0].start()

    for half in range(2):
        for slot in (NEAR, FAR):
            if half == 0:
                await_grads(half, slot)
            else:

                @pl.when(s >= slot)
                def _():
                    await_grads(half, slot)

        total = (
            grads_own[half]
            + grads_in[half, NEAR].astype(jnp.float32)
            + grads_in[half, FAR].astype(jnp.float32)
        ).astype(jnp.bfloat16)
        piece = pl.ds(half * PIECE, PIECE)
        dk_out[piece, :] = total[:, :HEAD_SIZE]
        dv_out[piece, :] = total[:, HEAD_SIZE:]
        for which, (made, to) in enumerate(((dk_out, dk_hbm), (dv_out, dv_hbm))):
            copy = pltpu.make_async_copy(made.at[piece], to.at[piece], store_sem.at[1 + 2 * half + which])
            copy.start()
            stores.append(copy)

    for wanted, copies in forward:

        @pl.when(wanted)
        def _():
            for copy in copies():
                copy.wait_send()

    for half in range(2):
        for wanted, copy in backward[half]:

            @pl.when(wanted)
            def _():
                copy().wait_send()

    for copy in stores:
        copy.wait()


def on_device(queries, keys, values, grad_out, starts):
    n = lax.axis_size("seq")
    bf16, f32 = jnp.bfloat16, jnp.float32
    vmem, dma = pltpu.VMEM, pltpu.SemaphoreType.DMA
    anywhere = pl.BlockSpec(memory_space=pl.ANY)
    return pl.pallas_call(
        functools.partial(kernel, n),
        out_shape=(
            jax.ShapeDtypeStruct(queries.shape, bf16),
            jax.ShapeDtypeStruct(keys.shape, bf16),
            jax.ShapeDtypeStruct(values.shape, bf16),
        ),
        in_specs=[anywhere] * 4 + [pl.BlockSpec(memory_space=pltpu.SMEM)],
        out_specs=(anywhere,) * 3,
        scratch_shapes=[
            vmem((2 * PIECE, 2 * HEAD_SIZE), bf16),
            vmem((2 * PIECE, 2 * HEAD_SIZE), bf16),
            vmem((2, 3, PIECE, HEAD_SIZE), bf16),
            vmem((2, 3, PIECE, HEAD_SIZE), bf16),
            vmem((2, 3, HEAD_SIZE, PIECE), bf16),
            vmem((2, 8, BLOCK), f32),
            vmem((2, 3, 8, BLOCK), f32),
            vmem((2, LANES, HEAD_SIZE), bf16),
            vmem((2, LANES, HEAD_SIZE), bf16),
            vmem((2, 3, PIECE, LANES), f32),
            vmem((2, 3, PIECE, LANES), f32),
            vmem((2, 3, PIECE, LANES), bf16),
            vmem((2, 3, 8, LANES), f32),
            vmem((2, 2, PIECE, 2 * HEAD_SIZE), bf16),
            vmem((2, 3, PIECE, 2 * HEAD_SIZE), bf16),
            vmem((2, PIECE, 2 * HEAD_SIZE), f32),
            vmem((2 * PIECE, 2 * HEAD_SIZE), bf16),
            vmem((2 * PIECE, HEAD_SIZE), bf16),
            vmem((2 * PIECE, HEAD_SIZE), bf16),
            dma((6,)),
            dma((5,)),
        ]
        + [dma((2, 2))] * 8,
        compiler_params=pltpu.CompilerParams(
            collective_id=0, has_side_effects=True, vmem_limit_bytes=58 << 20
        ),
    )(queries, grad_out, keys, values, starts)


def solution(mesh):
    in_specs = (P("seq", "head"), P("seq", "head"), P("seq", "head"), P("seq", "head"), P("seq"))
    out_specs = (P("seq", "head"), P("seq", "head"), P("seq", "head"))
    return jax.shard_map(
        on_device, mesh=mesh, in_specs=in_specs, out_specs=out_specs, check_vma=False
    )
```

time: 161 us -> 45.7 us (0.28)
  the two profiles are of different devices: /device:TPU:254 before, /device:TPU:480 now
where the time goes in v1:
time: 45.7 us; the launch traced here: 45.5 us
  Pallas kernels  41.2 us (90%)
  local copies, waits for them, and re-layouts  3.66 us (8%)
  between operations  0.65 us (1%)
    pallas_call x1, Pallas kernels, on_device(): pl.pallas_call(functools.partial(kernel, n), out_shape=(jax.ShapeDtypeStr...  41.2 us
    unnamed x7, local copies, waits for them, and re-layouts  3.66 us

profile of v1, /device:TPU:480, one launch (start us, length us, event | category | flops | bytes accessed | tf_op | source)
XLA Modules:
  0.0 45.5 jit_solution(17632625743377858592)
XLA Ops:
  0.6 41.2 %shard_map.76 = (bf16[1024,256]{1,0:T(8,128)(2,1)}, bf16[1024,128]{1,0:T(8,128)(2,1)}, bf16[1024,128]{1,0:T(8,128)(2,1)}) custom-call(bf16[1024,256]{1,0:T(8,128)(2,1)} %q_hbm.1, bf16[1024,256]{1,0:T(8,128)(2,1)} %g_hbm.1, bf16[1024,128]{1,0:T(8,128)(2,1)} %k_hbm.1, bf16[1024,128]{1,0:T(8,128)(2,1)} %v_hbm.1, s32[8]{0:T(128)} %starts.1), custom_call_target="tpu_custom_call" | custom-call | tf_op jit(solution)/shard_map/pallas_call | solution.py:340
  41.8 0.0 copy-start.1
  41.8 1.9 %copy.11 = bf16[1024,256]{1,0:T(8,128)(2,1)} copy(bf16[1024,256]{1,0:T(8,128)(2,1)} %get-tuple-element.6) | data formatting | bytes 1048576
  43.8 0.0 copy-done.1
  43.8 0.0 copy-start
  43.8 0.7 %copy.12 = bf16[1024,128]{1,0:T(8,128)(2,1)} copy(bf16[1024,128]{1,0:T(8,128)(2,1)S(1)} %copy-done.1) | data formatting | bytes 524288
  44.5 0.3 copy-done
  44.8 0.7 %copy.13 = bf16[1024,128]{1,0:T(8,128)(2,1)} copy(bf16[1024,128]{1,0:T(8,128)(2,1)S(1)} %copy-done) | data formatting | bytes 524288
Async XLA Ops:
  41.8 1.9 %copy-start.1 = (bf16[1024,128]{1,0:T(8,128)(2,1)S(1)}, bf16[1024,128]{1,0:T(8,128)(2,1)}, u32[]{:S(2)}) copy-start(bf16[1024,128]{1,0:T(8,128)(2,1)} %get-tuple-element.7) | copy-start | bytes 786436
  43.8 1.0 %copy-start = (bf16[1024,128]{1,0:T(8,128)(2,1)S(1)}, bf16[1024,128]{1,0:T(8,128)(2,1)}, u32[]{:S(2)}) copy-start(bf16[1024,128]{1,0:T(8,128)(2,1)} %get-tuple-element.8) | copy-start | bytes 786436

commit v2 on v1

--- a/solution.py
+++ b/solution.py
@@ -44,7 +44,7 @@
 
 def kernel(
     n, q_hbm, g_hbm, k_hbm, v_hbm, starts, dq_hbm, dk_hbm, dv_hbm,
-    q_in, g_in, k_all, v_all, k_t, table, tables, q_cat, g_cat, terms, dweights, dscores, stats,
+    q_in, g_in, k_all, v_all, k_t, table, tables, k_hop, q_cat, g_cat, terms, dweights, dscores, stats,
     grads_out, grads_in, grads_own, dq_out, dk_out, dv_out,
     load_sem, store_sem, k_send, v_send, t_send, k_recv, v_recv, t_recv, g_send, g_recv,
 ):
@@ -78,6 +78,10 @@
             after = after + jnp.where((line < j) | (line == BLOCKS), own[j], 0.0)
         table[half] = after
 
+    @pl.when(s == n - 2)
+    def _():
+        grads_in[0, FAR] = jnp.zeros((PIECE, 2 * HEAD_SIZE), jnp.bfloat16)
+
     @pl.when(s == 0)
     def _():
         k_all[0, NEAR] = jnp.zeros((PIECE, HEAD_SIZE), jnp.bfloat16)
@@ -96,39 +100,70 @@
 
     folded = s > n - 3
     beyond = jnp.where(folded, 2 * n - 3 - s, s + 2)
-    other_half = jnp.where(folded, 1, 0)
-    same_half = jnp.where(folded, 0, 1)
-
-    def pass_piece(half, slot, there, to_half):
+    at_fold = s == n - 1
+    odd = s % 2 == 1
+    first = jnp.where(odd, 0, 1)
+
+    def send_piece(sources, sinks, sends, recvs, there):
+        return [
+            pltpu.make_async_remote_copy(*refs, device_id=(there, head), device_id_type=MESH)
+            for refs in zip(sources, sinks, sends, recvs)
+        ]
+
+    def at(refs, *index):
+        return [ref.at[index] for ref in refs]
+
+    pieces, sends, recvs = (tables, k_all, v_all), (t_send, k_send, v_send), (t_recv, k_recv, v_recv)
+
+    def own_refs(half):
         piece = pl.ds(half * PIECE, PIECE)
-        target = dict(device_id=(there, head), device_id_type=MESH)
-        at = (half, slot - 1)
-        to = (to_half, slot - 1)
-        return [
-            pltpu.make_async_remote_copy(
-                table.at[half], tables.at[to_half, slot], t_send.at[at], t_recv.at[to], **target),
-            pltpu.make_async_remote_copy(
-                k_hbm.at[piece], k_all.at[to_half, slot], k_send.at[at], k_recv.at[to], **target),
-            pltpu.make_async_remote_copy(
-                v_hbm.at[piece], v_all.at[to_half, slot], v_send.at[at], v_recv.at[to], **target),
-        ]
+        return table.at[half], k_hbm.at[piece], v_hbm.at[piece]
+
+    def own_piece(half, slot, there):
+        return send_piece(
+            own_refs(half), at(pieces, half, slot), at(sends, half, slot - 1), at(recvs, half, slot - 1), there)
+
+    def held_piece(half, there):
+        return send_piece(
+            at(pieces, half, FAR), at(pieces, half, NEAR), at(sends, 2, 0), at(recvs, half, NEAR - 1), there)
+
+    def sidestep():
+        return pltpu.make_async_remote_copy(
+            own_refs(0)[1], k_hop, k_send.at[2, 1], k_recv.at[2, 0],
+            device_id=(n - 4, head), device_id_type=MESH)
+
+    def onward():
+        return pltpu.make_async_remote_copy(
+            k_hop, k_all.at[0, NEAR], k_send.at[2, 1], k_recv.at[0, NEAR - 1],
+            device_id=(n - 2, head), device_id_type=MESH)
+
+    def folded_piece():
+        return send_piece(
+            own_refs(0), at(pieces, 1, FAR), at(sends, 0, FAR - 1), at(recvs, 1, FAR - 1), n - 2)
 
     def pass_grads(half, slot, there, to_half):
         return pltpu.make_async_remote_copy(
             grads_out.at[half, slot - 1], grads_in.at[to_half, slot], g_send.at[half, slot - 1],
             g_recv.at[to_half, slot - 1], device_id=(there, head), device_id_type=MESH)
 
-    at_fold = s == n - 1
     forward = [
-        (s < n - 1, lambda: pass_piece(0, NEAR, s + 1, 0)),
-        (s >= 1, lambda: pass_piece(1, NEAR, s - 1, 1)),
-        (s >= 0, lambda: pass_piece(0, FAR, beyond, other_half)),
-        (s >= 2, lambda: pass_piece(1, FAR, s - 2, 1)),
+        (~odd, lambda: own_piece(0, NEAR, s + 1)),
+        (odd, lambda: own_piece(1, NEAR, s - 1)),
+        (at_fold, folded_piece),
+        (s == n - 3, lambda: [sidestep()]),
+        (s <= n - 3, lambda: own_piece(0, FAR, s + 2)),
+        (s >= 2, lambda: own_piece(1, FAR, s - 2)),
     ]
+    relays = jnp.where(odd, s >= 3, s <= n - 4)
+    relay = lambda: held_piece(jnp.where(odd, 0, 1), jnp.where(odd, s - 1, s + 1))
     across = [
         pltpu.make_async_copy(table.at[0], tables.at[1, NEAR], t_recv.at[1, 0]),
         pltpu.make_async_copy(k_hbm.at[pl.ds(0, PIECE)], k_all.at[1, NEAR], k_recv.at[1, 0]),
         pltpu.make_async_copy(v_hbm.at[pl.ds(0, PIECE)], v_all.at[1, NEAR], v_recv.at[1, 0]),
+    ]
+    again = [
+        pltpu.make_async_copy(kept.at[0, NEAR], kept.at[1, FAR], sem.at[1, 1])
+        for kept, sem in ((tables, t_recv), (k_all, k_recv), (v_all, v_recv))
     ]
     for wanted, copies in forward:
 
@@ -242,47 +277,93 @@
                 dq_out[rows, h * HEAD_SIZE : (h + 1) * HEAD_SIZE] = turned[h * BLOCK : (h + 1) * BLOCK, :]
 
     def await_piece(half, slot):
-        pltpu.make_async_copy(table.at[0], tables.at[half, slot], t_recv.at[half, slot - 1]).wait()
-        pltpu.make_async_copy(k_hbm.at[pl.ds(0, PIECE)], k_all.at[half, slot], k_recv.at[half, slot - 1]).wait()
-        pltpu.make_async_copy(v_hbm.at[pl.ds(0, PIECE)], v_all.at[half, slot], v_recv.at[half, slot - 1]).wait()
+        return [
+            pltpu.make_async_copy(*refs)
+            for refs in zip(own_refs(0), at(pieces, half, slot), at(recvs, half, slot - 1))
+        ]
 
     def await_grads(half, slot):
         pltpu.make_async_copy(grads_out.at[0, 0], grads_in.at[half, slot], g_recv.at[half, slot - 1]).wait()
 
+    def near_grads(half):
+        return pass_grads(half, NEAR, jnp.where(half == 0, s - 1, s + 1), half)
+
+    def far_grads(half):
+        there = jnp.where(half == 0, s - 2, beyond)
+        return pass_grads(half, FAR, there, jnp.where((half == 0) | folded, 0, 1))
+
+    def near_wanted(half):
+        return jnp.where(half == 0, s >= 1, s < n - 1)
+
+    def far_wanted(half):
+        return jnp.where(half == 0, s >= 2, s < n - 1)
+
+    home = pltpu.make_async_copy(grads_out.at[1, 0], grads_in.at[0, NEAR], g_recv.at[0, 0])
+
     for half in range(2):
         first_pass(half, OWN)
 
-    backward = [
-        [(s >= 1, lambda: pass_grads(0, NEAR, s - 1, 0)), (s >= 2, lambda: pass_grads(0, FAR, s - 2, 0))],
-        [(s < n - 1, lambda: pass_grads(1, NEAR, s + 1, 1)), (s >= 0, lambda: pass_grads(1, FAR, beyond, same_half))],
-    ]
-    home = pltpu.make_async_copy(grads_out.at[1, 0], grads_in.at[0, NEAR], g_recv.at[0, 0])
-
-    for half in range(2):
-        for slot in (NEAR, FAR):
-            if half == 1:
-                await_piece(half, slot)
-            else:
-
-                @pl.when(s >= slot)
+    def earlier_pieces(turn, carry):
+        half = jnp.where(turn == 0, first, 1 - first)
+
+        @pl.when((half == 1) | (s >= 2))
+        def _():
+            for which, (awaited, copy) in enumerate(zip(await_piece(half, FAR), relay())):
+                awaited.wait()
+                able = relays & ~at_fold if which == 1 else relays
+
+                @pl.when(able & (turn == 0))
                 def _():
-                    await_piece(half, slot)
-
-            first_pass(half, slot)
+                    copy.start()
+
+        @pl.when((s == n - 4) & (turn == 0))
+        def _():
+            pltpu.make_async_copy(own_refs(0)[1], k_hop, k_recv.at[2, 0]).wait()
+            onward().start()
+
+        @pl.when((half == 1) | (s >= 1))
+        def _():
+            await_piece(half, NEAR)[0].wait()
+
+        first_pass(half, FAR)
+
+        @pl.when((half == 1) | (s >= 1))
+        def _():
+            for copy in await_piece(half, NEAR)[1:]:
+                copy.wait()
+
+        @pl.when(at_fold & (turn == 0))
+        def _():
+            for copy in again:
+                copy.start()
+
+        first_pass(half, NEAR)
         merge(half)
-        for slot in (NEAR, FAR):
-            second_pass(half, slot)
-            wanted, copy = backward[half][slot - 1]
-
-            @pl.when(wanted)
-            def _():
-                copy().start()
-
-            if half == 1 and slot == NEAR:
-
-                @pl.when(at_fold)
-                def _():
-                    home.start()
+        second_pass(half, NEAR)
+
+        @pl.when(near_wanted(half) & ~(at_fold & (half == 0)))
+        def _():
+            near_grads(half).start()
+
+        @pl.when(at_fold & (half == 1))
+        def _():
+            home.start()
+
+        second_pass(half, FAR)
+
+        @pl.when(far_wanted(half))
+        def _():
+            far_grads(half).start()
+
+        @pl.when(at_fold & (half == 1))
+        def _():
+            both = grads_out[0, NEAR - 1].astype(jnp.float32) + grads_out[1, FAR - 1].astype(jnp.float32)
+            grads_out[0, NEAR - 1] = both.astype(jnp.bfloat16)
+            near_grads(0).start()
+
+        return carry
+
+    lax.fori_loop(0, 2, earlier_pieces, 0)
 
     stores = []
     for half in range(2):
@@ -291,28 +372,33 @@
     stores.append(pltpu.make_async_copy(dq_out, dq_hbm, store_sem.at[0]))
     stores[0].start()
 
-    for half in range(2):
+    def total_grads(turn, carry):
+        half = jnp.where(turn == 0, 1 - first, first)
         for slot in (NEAR, FAR):
-            if half == 0:
+
+            @pl.when(jnp.where(half == 0, s != (n - 2 if slot == FAR else n), s >= slot))
+            def _():
                 await_grads(half, slot)
-            else:
-
-                @pl.when(s >= slot)
-                def _():
-                    await_grads(half, slot)
 
         total = (
             grads_own[half]
             + grads_in[half, NEAR].astype(jnp.float32)
             + grads_in[half, FAR].astype(jnp.float32)
         ).astype(jnp.bfloat16)
+        dk_out[half] = total[:, :HEAD_SIZE]
+        dv_out[half] = total[:, HEAD_SIZE:]
+        for copy in grad_stores(half):
+            copy.start()
+        return carry
+
+    def grad_stores(half):
         piece = pl.ds(half * PIECE, PIECE)
-        dk_out[piece, :] = total[:, :HEAD_SIZE]
-        dv_out[piece, :] = total[:, HEAD_SIZE:]
-        for which, (made, to) in enumerate(((dk_out, dk_hbm), (dv_out, dv_hbm))):
-            copy = pltpu.make_async_copy(made.at[piece], to.at[piece], store_sem.at[1 + 2 * half + which])
-            copy.start()
-            stores.append(copy)
+        return [
+            pltpu.make_async_copy(dk_out.at[half], dk_hbm.at[piece], store_sem.at[1 + half]),
+            pltpu.make_async_copy(dv_out.at[half], dv_hbm.at[piece], store_sem.at[3 + half]),
+        ]
+
+    lax.fori_loop(0, 2, total_grads, 0)
 
     for wanted, copies in forward:
 
@@ -321,15 +407,37 @@
             for copy in copies():
                 copy.wait_send()
 
-    for half in range(2):
-        for wanted, copy in backward[half]:
-
-            @pl.when(wanted)
-            def _():
-                copy().wait_send()
+    for which, copy in enumerate(relay()):
+
+        @pl.when(relays & ~at_fold if which == 1 else relays)
+        def _():
+            copy.wait_send()
+
+    @pl.when(s == n - 4)
+    def _():
+        onward().wait_send()
+
+    for half in range(2):
+
+        @pl.when(near_wanted(half))
+        def _():
+            near_grads(half).wait_send()
+
+        @pl.when(far_wanted(half))
+        def _():
+            far_grads(half).wait_send()
+
+        for copy in grad_stores(half):
+            copy.wait()
 
     for copy in stores:
         copy.wait()
+
+
+def store_kernel(dq_ref, dk_ref, dv_ref, dq_out, dk_out, dv_out):
+    dq_out[...] = dq_ref[...]
+    dk_out[...] = dk_ref[...]
+    dv_out[...] = dv_ref[...]
 
 
 def on_device(queries, keys, values, grad_out, starts):
@@ -337,13 +445,14 @@
     bf16, f32 = jnp.bfloat16, jnp.float32
     vmem, dma = pltpu.VMEM, pltpu.SemaphoreType.DMA
     anywhere = pl.BlockSpec(memory_space=pl.ANY)
-    return pl.pallas_call(
+    shapes = (
+        jax.ShapeDtypeStruct(queries.shape, bf16),
+        jax.ShapeDtypeStruct(keys.shape, bf16),
+        jax.ShapeDtypeStruct(values.shape, bf16),
+    )
+    made = pl.pallas_call(
         functools.partial(kernel, n),
-        out_shape=(
-            jax.ShapeDtypeStruct(queries.shape, bf16),
-            jax.ShapeDtypeStruct(keys.shape, bf16),
-            jax.ShapeDtypeStruct(values.shape, bf16),
-        ),
+        out_shape=shapes,
         in_specs=[anywhere] * 4 + [pl.BlockSpec(memory_space=pltpu.SMEM)],
         out_specs=(anywhere,) * 3,
         scratch_shapes=[
@@ -354,6 +463,7 @@
             vmem((2, 3, HEAD_SIZE, PIECE), bf16),
             vmem((2, 8, BLOCK), f32),
             vmem((2, 3, 8, BLOCK), f32),
+            vmem((PIECE, HEAD_SIZE), bf16),
             vmem((2, LANES, HEAD_SIZE), bf16),
             vmem((2, LANES, HEAD_SIZE), bf16),
             vmem((2, 3, PIECE, LANES), f32),
@@ -364,16 +474,18 @@
             vmem((2, 3, PIECE, 2 * HEAD_SIZE), bf16),
             vmem((2, PIECE, 2 * HEAD_SIZE), f32),
             vmem((2 * PIECE, 2 * HEAD_SIZE), bf16),
-            vmem((2 * PIECE, HEAD_SIZE), bf16),
-            vmem((2 * PIECE, HEAD_SIZE), bf16),
+            vmem((2, PIECE, HEAD_SIZE), bf16),
+            vmem((2, PIECE, HEAD_SIZE), bf16),
             dma((6,)),
             dma((5,)),
         ]
-        + [dma((2, 2))] * 8,
+        + [dma((3, 2))] * 6 + [dma((2, 2))] * 2,
         compiler_params=pltpu.CompilerParams(
             collective_id=0, has_side_effects=True, vmem_limit_bytes=58 << 20
         ),
     )(queries, grad_out, keys, values, starts)
+    whole = pl.BlockSpec(memory_space=pltpu.VMEM)
+    return pl.pallas_call(store_kernel, out_shape=shapes, in_specs=[whole] * 3, out_specs=(whole,) * 3)(*made)
 
 
 def solution(mesh):

time: 45.7 us -> 39.8 us (0.87)
  the two profiles are of different devices: /device:TPU:480 before, /device:TPU:472 now
where the time goes in v2:
time: 39.8 us; the launch traced here: 39.6 us
  Pallas kernels  39 us (98%)
  between operations  0.64 us (2%)
    pallas_call x1, Pallas kernels, on_device(): pl.pallas_call(functools.partial(kernel, n), out_shape=shapes, in_specs=[...  36.8 us
    pallas_call x1, Pallas kernels, on_device(): pl.pallas_call(store_kernel, out_shape=shapes, in_specs=[whole] * 3, out_...  2.17 us

profile of v2, /device:TPU:472, one launch (start us, length us, event | category | flops | bytes accessed | tf_op | source)
XLA Modules:
  0.0 39.6 jit_solution(7113529419330252695)
XLA Ops:
  0.6 36.8 %shard_map.76 = (bf16[1024,256]{1,0:T(8,128)(2,1)}, bf16[1024,128]{1,0:T(8,128)(2,1)}, bf16[1024,128]{1,0:T(8,128)(2,1)}) custom-call(bf16[1024,256]{1,0:T(8,128)(2,1)} %q_hbm.1, bf16[1024,256]{1,0:T(8,128)(2,1)} %g_hbm.1, bf16[1024,128]{1,0:T(8,128)(2,1)} %k_hbm.1, bf16[1024,128]{1,0:T(8,128)(2,1)} %v_hbm.1, s32[8]{0:T(128)} %starts.1), custom_call_target="tpu_custom_call" | custom-call | tf_op jit(solution)/shard_map/pallas_call | solution.py:453
  37.4 2.2 %shard_map.77 = (bf16[1024,256]{1,0:T(8,128)(2,1)}, bf16[1024,128]{1,0:T(8,128)(2,1)}, bf16[1024,128]{1,0:T(8,128)(2,1)}) custom-call(bf16[1024,256]{1,0:T(8,128)(2,1)} %get-tuple-element.6.dq_ref, bf16[1024,128]{1,0:T(8,128)(2,1)} %get-tuple-element.7.dk_ref, bf16[1024,128]{1,0:T(8,128)(2,1)} %get-tuple-element.8.dv_ref), custom_call_target="tpu_custom_call" | custom-call | tf_op jit(solution)/shard_map/pallas_call | solution.py:488

commit v3 on v2

--- a/solution.py
+++ b/solution.py
@@ -43,10 +43,10 @@
 
 
 def kernel(
-    n, q_hbm, g_hbm, k_hbm, v_hbm, starts, dq_hbm, dk_hbm, dv_hbm,
+    n, q_hbm, g_hbm, k_hbm, v_hbm, starts, dq_out, dk_out, dv_out,
     q_in, g_in, k_all, v_all, k_t, table, tables, k_hop, q_cat, g_cat, terms, dweights, dscores, stats,
-    grads_out, grads_in, grads_own, dq_out, dk_out, dv_out,
-    load_sem, store_sem, k_send, v_send, t_send, k_recv, v_recv, t_recv, g_send, g_recv,
+    grads_out, grads_in, grads_own,
+    load_sem, k_send, v_send, t_send, k_recv, v_recv, t_recv, g_send, g_recv,
 ):
     s = lax.axis_index("seq")
     head = lax.axis_index("head")
@@ -365,12 +365,9 @@
 
     lax.fori_loop(0, 2, earlier_pieces, 0)
 
-    stores = []
     for half in range(2):
         second_pass(half, OWN)
         query_pass(half)
-    stores.append(pltpu.make_async_copy(dq_out, dq_hbm, store_sem.at[0]))
-    stores[0].start()
 
     def total_grads(turn, carry):
         half = jnp.where(turn == 0, 1 - first, first)
@@ -385,18 +382,10 @@
             + grads_in[half, NEAR].astype(jnp.float32)
             + grads_in[half, FAR].astype(jnp.float32)
         ).astype(jnp.bfloat16)
-        dk_out[half] = total[:, :HEAD_SIZE]
-        dv_out[half] = total[:, HEAD_SIZE:]
-        for copy in grad_stores(half):
-            copy.start()
+        piece = pl.ds(pl.multiple_of(half * PIECE, PIECE), PIECE)
+        dk_out[piece, :] = total[:, :HEAD_SIZE]
+        dv_out[piece, :] = total[:, HEAD_SIZE:]
         return carry
-
-    def grad_stores(half):
-        piece = pl.ds(half * PIECE, PIECE)
-        return [
-            pltpu.make_async_copy(dk_out.at[half], dk_hbm.at[piece], store_sem.at[1 + half]),
-            pltpu.make_async_copy(dv_out.at[half], dv_hbm.at[piece], store_sem.at[3 + half]),
-        ]
 
     lax.fori_loop(0, 2, total_grads, 0)
 
@@ -427,17 +416,17 @@
         def _():
             far_grads(half).wait_send()
 
-        for copy in grad_stores(half):
-            copy.wait()
-
-    for copy in stores:
+
+def store_kernel(dq_ref, dk_ref, dv_ref, dq_hbm, dk_hbm, dv_hbm, sems):
+    copies = []
+    for which, (made, to) in enumerate(((dq_ref, dq_hbm), (dk_ref, dk_hbm), (dv_ref, dv_hbm))):
+        for half in range(2):
+            piece = pl.ds(half * PIECE, PIECE)
+            copies.append(pltpu.make_async_copy(made.at[piece], to.at[piece], sems.at[2 * which + half]))
+    for copy in copies:
+        copy.start()
+    for copy in copies:
         copy.wait()
-
-
-def store_kernel(dq_ref, dk_ref, dv_ref, dq_out, dk_out, dv_out):
-    dq_out[...] = dq_ref[...]
-    dk_out[...] = dk_ref[...]
-    dv_out[...] = dv_ref[...]
 
 
 def on_device(queries, keys, values, grad_out, starts):
@@ -454,7 +443,7 @@
         functools.partial(kernel, n),
         out_shape=shapes,
         in_specs=[anywhere] * 4 + [pl.BlockSpec(memory_space=pltpu.SMEM)],
-        out_specs=(anywhere,) * 3,
+        out_specs=(pl.BlockSpec(memory_space=pltpu.VMEM),) * 3,
         scratch_shapes=[
             vmem((2 * PIECE, 2 * HEAD_SIZE), bf16),
             vmem((2 * PIECE, 2 * HEAD_SIZE), bf16),
@@ -473,19 +462,21 @@
             vmem((2, 2, PIECE, 2 * HEAD_SIZE), bf16),
             vmem((2, 3, PIECE, 2 * HEAD_SIZE), bf16),
             vmem((2, PIECE, 2 * HEAD_SIZE), f32),
-            vmem((2 * PIECE, 2 * HEAD_SIZE), bf16),
-            vmem((2, PIECE, HEAD_SIZE), bf16),
-            vmem((2, PIECE, HEAD_SIZE), bf16),
             dma((6,)),
-            dma((5,)),
         ]
         + [dma((3, 2))] * 6 + [dma((2, 2))] * 2,
         compiler_params=pltpu.CompilerParams(
-            collective_id=0, has_side_effects=True, vmem_limit_bytes=58 << 20
+            collective_id=0, has_side_effects=True, vmem_limit_bytes=48 << 20
         ),
-    )(queries, grad_out, keys, values, starts)
-    whole = pl.BlockSpec(memory_space=pltpu.VMEM)
-    return pl.pallas_call(store_kernel, out_shape=shapes, in_specs=[whole] * 3, out_specs=(whole,) * 3)(*made)
+    )(*(pltpu.with_memory_space_constraint(x, pltpu.HBM) for x in (queries, grad_out, keys, values, starts)))
+    return pl.pallas_call(
+        store_kernel,
+        out_shape=shapes,
+        in_specs=[anywhere] * 3,
+        out_specs=(pl.BlockSpec(memory_space=pltpu.HBM),) * 3,
+        scratch_shapes=[dma((6,))],
+        compiler_params=pltpu.CompilerParams(vmem_limit_bytes=1 << 20),
+    )(*made)
 
 
 def solution(mesh):

time: 39.8 us -> 37.9 us (0.952)
  Pallas kernels: 39 us -> 37.1 us
    pallas_call x1, Pallas kernels: 2.17 us -> 1.01 us  [on_device(): pl.pallas_call(store_kernel, out_shape=shapes, in_specs=[anywhere] * 3, o...]
    pallas_call x1, Pallas kernels: 36.8 us -> 36.1 us  [on_device(): pl.pallas_call(functools.partial(kernel, n), out_shape=shapes, in_specs=[...]
where the time goes in v3:
time: 37.9 us; the launch traced here: 37.8 us
  Pallas kernels  37.1 us (98%)
  between operations  0.64 us (2%)
    pallas_call x1, Pallas kernels, on_device(): pl.pallas_call(functools.partial(kernel, n), out_shape=shapes, in_specs=[...  36.1 us
    pallas_call x1, Pallas kernels, on_device(): pl.pallas_call(store_kernel, out_shape=shapes, in_specs=[anywhere] * 3, o...  1.01 us

profile of v3, /device:TPU:472, one launch (start us, length us, event | category | flops | bytes accessed | tf_op | source)
XLA Modules:
  0.0 37.8 jit_solution(13403697788661349732)
XLA Ops:
  0.6 36.1 %shard_map.76 = (bf16[1024,256]{1,0:T(8,128)(2,1)S(1)}, bf16[1024,128]{1,0:T(8,128)(2,1)S(1)}, bf16[1024,128]{1,0:T(8,128)(2,1)S(1)}) custom-call(bf16[1024,256]{1,0:T(8,128)(2,1)} %q_hbm.1, bf16[1024,256]{1,0:T(8,128)(2,1)} %g_hbm.1, bf16[1024,128]{1,0:T(8,128)(2,1)} %k_hbm.1, bf16[1024,128]{1,0:T(8,128)(2,1)} %v_hbm.1, s32[8]{0:T(128)} %starts.1), custom_call_target="tpu_custom_call" | custom-call | tf_op jit(solution)/shard_map/pallas_call | solution.py:442
  36.8 1.0 %shard_map.77 = (bf16[1024,256]{1,0:T(8,128)(2,1)}, bf16[1024,128]{1,0:T(8,128)(2,1)}, bf16[1024,128]{1,0:T(8,128)(2,1)}) custom-call(bf16[1024,256]{1,0:T(8,128)(2,1)S(1)} %get-tuple-element.6.dq_ref, bf16[1024,128]{1,0:T(8,128)(2,1)S(1)} %get-tuple-element.7.dk_ref, bf16[1024,128]{1,0:T(8,128)(2,1)S(1)} %get-tuple-element.8.dv_ref), custom_call_target="tpu_custom_call" | custom-call | tf_op jit(solution)/shard_map/pallas_call | solution.py:472

commit v4 on v3

--- a/solution.py
+++ b/solution.py
@@ -45,7 +45,7 @@
 def kernel(
     n, q_hbm, g_hbm, k_hbm, v_hbm, starts, dq_out, dk_out, dv_out,
     q_in, g_in, k_all, v_all, k_t, table, tables, k_hop, q_cat, g_cat, terms, dweights, dscores, stats,
-    grads_out, grads_in, grads_own,
+    grads_out, grads_in, grads_own, g_hop,
     load_sem, k_send, v_send, t_send, k_recv, v_recv, t_recv, g_send, g_recv,
 ):
     s = lax.axis_index("seq")
@@ -193,12 +193,11 @@
     query_row = lax.broadcasted_iota(jnp.int32, (BLOCK, TILE), 1) % BLOCK
     causal = key_row <= query_row
 
-    def first_pass(half, chunk):
+    def key_pass(half, chunk):
         k_t[half, chunk] = k_all[half, chunk].T
         for i in range(BLOCKS):
             begun = [starts[half * BLOCKS + j] for j in range(BLOCKS)]
             q_i = q_cat[half, lanes_of(i), :]
-            g_i = g_cat[half, lanes_of(i), :]
             scores = []
             for j in span(chunk, i):
                 x = last_dims(k_all[half, chunk, rows_of(j), :], q_i) * exp2_scaling
@@ -220,17 +219,26 @@
                 scores.append(x)
             top = functools.reduce(jnp.maximum, [jnp.max(x, axis=0, keepdims=True) for x in scores])
             total = jnp.zeros((1, TILE), jnp.float32)
-            dotted = jnp.zeros((1, TILE), jnp.float32)
             for j, x in zip(span(chunk, i), scores):
                 e = jnp.exp2(x - top)
-                w = last_dims(v_all[half, chunk, rows_of(j), :], g_i)
                 total = total + jnp.sum(e, axis=0, keepdims=True)
-                dotted = dotted + jnp.sum(e * w, axis=0, keepdims=True)
                 terms[half, chunk, rows_of(j), lanes_of(i)] = e
-                dweights[half, chunk, rows_of(j), lanes_of(i)] = w
             stats[half, chunk, 0:1, lanes_of(i)] = top
             stats[half, chunk, 1:2, lanes_of(i)] = total
+
+    def value_pass(half, chunk):
+        for i in range(BLOCKS):
+            g_i = g_cat[half, lanes_of(i), :]
+            dotted = jnp.zeros((1, TILE), jnp.float32)
+            for j in span(chunk, i):
+                w = last_dims(v_all[half, chunk, rows_of(j), :], g_i)
+                dotted = dotted + jnp.sum(terms[half, chunk, rows_of(j), lanes_of(i)] * w, axis=0, keepdims=True)
+                dweights[half, chunk, rows_of(j), lanes_of(i)] = w
             stats[half, chunk, 2:3, lanes_of(i)] = dotted
+
+    def first_pass(half, chunk):
+        key_pass(half, chunk)
+        value_pass(half, chunk)
 
     def merge(half):
         tops = [stats[half, c, 0:1, :] for c in range(3)]
@@ -243,8 +251,8 @@
             stats[half, c, 3:4, :] = ratios[c] * inverse
         stats[half, OWN, 4:5, :] = dotted * inverse
 
-    def second_pass(half, chunk):
-        for j in range(BLOCKS):
+    def second_pass(half, chunk, blocks=range(BLOCKS)):
+        for j in blocks:
             dk = jnp.zeros((BLOCK, HEAD_SIZE), jnp.float32)
             dv = jnp.zeros((BLOCK, HEAD_SIZE), jnp.float32)
             for i in range(BLOCKS):
@@ -282,11 +290,23 @@
             for refs in zip(own_refs(0), at(pieces, half, slot), at(recvs, half, slot - 1))
         ]
 
+    def await_near(half):
+        for part in range(2):
+            rows = part_rows(part)
+            pltpu.make_async_copy(
+                grads_out.at[0, 0, rows], grads_in.at[half, NEAR, rows], g_recv.at[2 * part + half, 0]).wait()
+
     def await_grads(half, slot):
         pltpu.make_async_copy(grads_out.at[0, 0], grads_in.at[half, slot], g_recv.at[half, slot - 1]).wait()
 
-    def near_grads(half):
-        return pass_grads(half, NEAR, jnp.where(half == 0, s - 1, s + 1), half)
+    def part_rows(part):
+        return pl.ds(part * (PIECE // 2), PIECE // 2)
+
+    def near_grads(half, part):
+        rows = part_rows(part)
+        return pltpu.make_async_remote_copy(
+            grads_out.at[half, NEAR - 1, rows], grads_in.at[half, NEAR, rows], g_send.at[2 * part + half, 0],
+            g_recv.at[2 * part + half, 0], device_id=(jnp.where(half == 0, s - 1, s + 1), head), device_id_type=MESH)
 
     def far_grads(half):
         there = jnp.where(half == 0, s - 2, beyond)
@@ -298,7 +318,22 @@
     def far_wanted(half):
         return jnp.where(half == 0, s >= 2, s < n - 1)
 
-    home = pltpu.make_async_copy(grads_out.at[1, 0], grads_in.at[0, NEAR], g_recv.at[0, 0])
+    def near_aside():
+        return pltpu.make_async_remote_copy(
+            grads_out.at[0, NEAR - 1, part_rows(1)], g_hop, g_send.at[2, 1], g_recv.at[2, 1],
+            device_id=(n - 1, head), device_id_type=MESH)
+
+    def near_onward():
+        return pltpu.make_async_remote_copy(
+            g_hop, grads_in.at[0, NEAR, part_rows(1)], g_send.at[3, 1], g_recv.at[2, 0],
+            device_id=(n - 3, head), device_id_type=MESH)
+
+    before_fold = s == n - 2
+
+    def home(part):
+        rows = part_rows(part)
+        return pltpu.make_async_copy(
+            grads_out.at[1, NEAR - 1, rows], grads_in.at[0, NEAR, rows], g_recv.at[2 * part, 0])
 
     for half in range(2):
         first_pass(half, OWN)
@@ -329,37 +364,56 @@
 
         @pl.when((half == 1) | (s >= 1))
         def _():
-            for copy in await_piece(half, NEAR)[1:]:
-                copy.wait()
+            await_piece(half, NEAR)[1].wait()
+
+        key_pass(half, NEAR)
+
+        @pl.when((half == 1) | (s >= 1))
+        def _():
+            await_piece(half, NEAR)[2].wait()
 
         @pl.when(at_fold & (turn == 0))
         def _():
             for copy in again:
                 copy.start()
 
-        first_pass(half, NEAR)
+        value_pass(half, NEAR)
         merge(half)
-        second_pass(half, NEAR)
-
-        @pl.when(near_wanted(half) & ~(at_fold & (half == 0)))
-        def _():
-            near_grads(half).start()
-
-        @pl.when(at_fold & (half == 1))
-        def _():
-            home.start()
-
-        second_pass(half, FAR)
-
-        @pl.when(far_wanted(half))
-        def _():
-            far_grads(half).start()
+        def near_block():
+            for part in range(2):
+                second_pass(half, NEAR, range(part * BLOCKS // 2, (part + 1) * BLOCKS // 2))
+
+                through = before_fold & (half == 0) & (part == 1)
+
+                @pl.when(near_wanted(half) & ~(at_fold & (half == 0)) & ~through)
+                def _():
+                    near_grads(half, part).start()
+
+                @pl.when(through)
+                def _():
+                    near_aside().start()
+                    far_grads(1).start()
+
+                @pl.when(at_fold & (half == 1))
+                def _():
+                    home(part).start()
+
+        def far_block():
+            second_pass(half, FAR)
+
+            @pl.when(far_wanted(half) & ~(before_fold & (half == 1)))
+            def _():
+                far_grads(half).start()
+
+        near_block()
+        far_block()
 
         @pl.when(at_fold & (half == 1))
         def _():
             both = grads_out[0, NEAR - 1].astype(jnp.float32) + grads_out[1, FAR - 1].astype(jnp.float32)
             grads_out[0, NEAR - 1] = both.astype(jnp.bfloat16)
-            near_grads(0).start()
+            for part in range(2):
+                near_grads(0, part).start()
 
         return carry
 
@@ -369,13 +423,20 @@
         second_pass(half, OWN)
         query_pass(half)
 
+    @pl.when(at_fold)
+    def _():
+        pltpu.make_async_copy(grads_out.at[0, 0, part_rows(0)], g_hop, g_recv.at[2, 1]).wait()
+        near_onward().start()
+
     def total_grads(turn, carry):
         half = jnp.where(turn == 0, 1 - first, first)
-        for slot in (NEAR, FAR):
-
-            @pl.when(jnp.where(half == 0, s != (n - 2 if slot == FAR else n), s >= slot))
-            def _():
-                await_grads(half, slot)
+        @pl.when((half == 0) | (s >= 1))
+        def _():
+            await_near(half)
+
+        @pl.when(jnp.where(half == 0, s != n - 2, s >= 2))
+        def _():
+            await_grads(half, FAR)
 
         total = (
             grads_own[half]
@@ -406,11 +467,25 @@
     def _():
         onward().wait_send()
 
+    @pl.when(at_fold)
+    def _():
+        near_onward().wait_send()
+
     for half in range(2):
 
         @pl.when(near_wanted(half))
         def _():
-            near_grads(half).wait_send()
+            near_grads(half, 0).wait_send()
+
+        through = before_fold & (half == 0)
+
+        @pl.when(near_wanted(half) & ~through)
+        def _():
+            near_grads(half, 1).wait_send()
+
+        @pl.when(through)
+        def _():
+            near_aside().wait_send()
 
         @pl.when(far_wanted(half))
         def _():
@@ -462,9 +537,10 @@
             vmem((2, 2, PIECE, 2 * HEAD_SIZE), bf16),
             vmem((2, 3, PIECE, 2 * HEAD_SIZE), bf16),
             vmem((2, PIECE, 2 * HEAD_SIZE), f32),
+            vmem((PIECE // 2, 2 * HEAD_SIZE), bf16),
             dma((6,)),
         ]
-        + [dma((3, 2))] * 6 + [dma((2, 2))] * 2,
+        + [dma((3, 2))] * 6 + [dma((4, 2))] * 2,
         compiler_params=pltpu.CompilerParams(
             collective_id=0, has_side_effects=True, vmem_limit_bytes=48 << 20
         ),

time: 37.9 us -> 37.1 us (0.979)
  the two profiles are of different devices: /device:TPU:472 before, /device:TPU:486 now
where the time goes in v4:
time: 37.1 us; the launch traced here: 37 us
  Pallas kernels  36.3 us (98%)
  between operations  0.64 us (2%)
    pallas_call x1, Pallas kernels, on_device(): pl.pallas_call(functools.partial(kernel, n), out_shape=shapes, in_specs=[...  35.3 us
    pallas_call x1, Pallas kernels, on_device(): pl.pallas_call(store_kernel, out_shape=shapes, in_specs=[anywhere] * 3, o...  1.01 us

profile of v4, /device:TPU:486, one launch (start us, length us, event | category | flops | bytes accessed | tf_op | source)
XLA Modules:
  0.0 37.0 jit_solution(3954267466262928645)
XLA Ops:
  0.6 35.3 %shard_map.76 = (bf16[1024,256]{1,0:T(8,128)(2,1)S(1)}, bf16[1024,128]{1,0:T(8,128)(2,1)S(1)}, bf16[1024,128]{1,0:T(8,128)(2,1)S(1)}) custom-call(bf16[1024,256]{1,0:T(8,128)(2,1)} %q_hbm.1, bf16[1024,256]{1,0:T(8,128)(2,1)} %g_hbm.1, bf16[1024,128]{1,0:T(8,128)(2,1)} %k_hbm.1, bf16[1024,128]{1,0:T(8,128)(2,1)} %v_hbm.1, s32[8]{0:T(128)} %starts.1), custom_call_target="tpu_custom_call" | custom-call | tf_op jit(solution)/shard_map/pallas_call | solution.py:517
  36.0 1.0 %shard_map.77 = (bf16[1024,256]{1,0:T(8,128)(2,1)}, bf16[1024,128]{1,0:T(8,128)(2,1)}, bf16[1024,128]{1,0:T(8,128)(2,1)}) custom-call(bf16[1024,256]{1,0:T(8,128)(2,1)S(1)} %get-tuple-element.6.dq_ref, bf16[1024,128]{1,0:T(8,128)(2,1)S(1)} %get-tuple-element.7.dk_ref, bf16[1024,128]{1,0:T(8,128)(2,1)S(1)} %get-tuple-element.8.dv_ref), custom_call_target="tpu_custom_call" | custom-call | tf_op jit(solution)/shard_map/pallas_call | solution.py:548

commit v5 on v4

--- a/solution.py
+++ b/solution.py
@@ -11,6 +11,7 @@
 BLOCK = 128
 PIECE = 512
 BLOCKS = PIECE // BLOCK
+LARGER = 3
 HEADS = 2
 TILE = HEADS * BLOCK
 LANES = BLOCKS * TILE
@@ -300,7 +301,7 @@
         pltpu.make_async_copy(grads_out.at[0, 0], grads_in.at[half, slot], g_recv.at[half, slot - 1]).wait()
 
     def part_rows(part):
-        return pl.ds(part * (PIECE // 2), PIECE // 2)
+        return pl.ds(LARGER * BLOCK, PIECE - LARGER * BLOCK) if part else pl.ds(0, LARGER * BLOCK)
 
     def near_grads(half, part):
         rows = part_rows(part)
@@ -381,7 +382,7 @@
         merge(half)
         def near_block():
             for part in range(2):
-                second_pass(half, NEAR, range(part * BLOCKS // 2, (part + 1) * BLOCKS // 2))
+                second_pass(half, NEAR, range(LARGER, BLOCKS) if part else range(LARGER))
 
                 through = before_fold & (half == 0) & (part == 1)
 
@@ -425,7 +426,7 @@
 
     @pl.when(at_fold)
     def _():
-        pltpu.make_async_copy(grads_out.at[0, 0, part_rows(0)], g_hop, g_recv.at[2, 1]).wait()
+        pltpu.make_async_copy(grads_out.at[0, 0, part_rows(1)], g_hop, g_recv.at[2, 1]).wait()
         near_onward().start()
 
     def total_grads(turn, carry):
@@ -537,7 +538,7 @@
             vmem((2, 2, PIECE, 2 * HEAD_SIZE), bf16),
             vmem((2, 3, PIECE, 2 * HEAD_SIZE), bf16),
             vmem((2, PIECE, 2 * HEAD_SIZE), f32),
-            vmem((PIECE // 2, 2 * HEAD_SIZE), bf16),
+            vmem((PIECE - LARGER * BLOCK, 2 * HEAD_SIZE), bf16),
             dma((6,)),
         ]
         + [dma((3, 2))] * 6 + [dma((4, 2))] * 2,

time: 37.1 us -> 36.9 us (level)
  the two profiles are of different devices: /device:TPU:486 before, /device:TPU:472 now
where the time goes in v5:
time: 36.9 us; the launch traced here: 36.7 us
  Pallas kernels  36.1 us (98%)
  between operations  0.64 us (2%)
    pallas_call x1, Pallas kernels, on_device(): pl.pallas_call(functools.partial(kernel, n), out_shape=shapes, in_specs=[...  35.1 us
    pallas_call x1, Pallas kernels, on_device(): pl.pallas_call(store_kernel, out_shape=shapes, in_specs=[anywhere] * 3, o...  1.01 us

profile of v5, /device:TPU:472, one launch (start us, length us, event | category | flops | bytes accessed | tf_op | source)
XLA Modules:
  0.0 36.7 jit_solution(17779920745768921529)
XLA Ops:
  0.6 35.1 %shard_map.76 = (bf16[1024,256]{1,0:T(8,128)(2,1)S(1)}, bf16[1024,128]{1,0:T(8,128)(2,1)S(1)}, bf16[1024,128]{1,0:T(8,128)(2,1)S(1)}) custom-call(bf16[1024,256]{1,0:T(8,128)(2,1)} %q_hbm.1, bf16[1024,256]{1,0:T(8,128)(2,1)} %g_hbm.1, bf16[1024,128]{1,0:T(8,128)(2,1)} %k_hbm.1, bf16[1024,128]{1,0:T(8,128)(2,1)} %v_hbm.1, s32[8]{0:T(128)} %starts.1), custom_call_target="tpu_custom_call" | custom-call | tf_op jit(solution)/shard_map/pallas_call | solution.py:518
  35.7 1.0 %shard_map.77 = (bf16[1024,256]{1,0:T(8,128)(2,1)}, bf16[1024,128]{1,0:T(8,128)(2,1)}, bf16[1024,128]{1,0:T(8,128)(2,1)}) custom-call(bf16[1024,256]{1,0:T(8,128)(2,1)S(1)} %get-tuple-element.6.dq_ref, bf16[1024,128]{1,0:T(8,128)(2,1)S(1)} %get-tuple-element.7.dk_ref, bf16[1024,128]{1,0:T(8,128)(2,1)S(1)} %get-tuple-element.8.dv_ref), custom_call_target="tpu_custom_call" | custom-call | tf_op jit(solution)/shard_map/pallas_call | solution.py:549
